TPU v7x, 512 devices: a whole 4x4x16 slice. The times are simulated.
512 devices in a mesh: along: 16 (over z), across: 32 (over x, y, core).
Axes of the slice: x: 4, y: 4, z: 16, core: 2. Of those that a mesh axis runs over, the one named last changes fastest.
Arguments:
- toa: bfloat16 [6, 3072, 8192], P(None, 'along', 'across'), may hold values from 0.015 to 1.21
- aot_seed: float32 [96, 256], P('along', 'across'), may hold values from 0.05 to 0.8
- valid: int32 [96, 256], P('along', 'across'), may hold values 0 or 1
- cloud: int32 [96, 256], P('along', 'across'), may hold values 0 or 1
- land_class: int32 [96, 256], P('along', 'across'), may hold values from 0 to 2
- row_taps: float32 [6, 3, 201], replicated, may hold values from 0.0015 to 1.31, as said below
- col_taps: float32 [6, 3, 201], replicated, may hold values from 0.0015 to 1.31, as said below
- tau: float32 [6], replicated, may hold values from 0.4 to 1.6
- adjacency: float32 [6], replicated, may hold values from 0.5 to 1.5
Outputs:
- surface: float32 [6, 3072, 8192], P(None, 'along', 'across')
Inputs may be any that keep to these rules, and one draw needn't show every extreme that they name: `row_taps`: positive taps. `col_taps`: positive taps.
All inputs are finite; a program needn't handle non-finite values. No bound on the sum of `valid` or of `cloud` on one device may be relied on, other than what follows from the above.
Results may differ from a plain program's by a relative error of at most 0.00055.
Values may be sent and summed in bfloat16 or wider, within the bound.
No kernel may reach another device: no remote copies, remote signals or barrier semaphores. Data moves between devices by JAX's collectives and lax.ppermute only.
A program may use at most 64 MiB of HBM per device.

v0:
```python
import jax
import jax.numpy as jnp
from jax import lax
from jax.experimental import pallas as pl
from jax.experimental.pallas import tpu as pltpu
from jax.sharding import PartitionSpec as P

BANDS = 6
KR = 100
TAPS = 201
CB = 32
SWEEPS = 4
ROWS = 192
COLS = 256
HALO = 104
SIDE = 128
CELL_ROWS = 6
CELL_COLS = 8
UNROLL_OWN = False
UNROLL_LAST = True
F32 = jnp.float32
BF16 = jnp.bfloat16
VMEM = pl.BlockSpec(memory_space=pltpu.VMEM)
SMEM = pl.BlockSpec(memory_space=pltpu.SMEM)


def iota(shape, dim):
    return lax.broadcasted_iota(jnp.int32, shape, dim)


def shift(value, axis, step):
    count = lax.axis_size(axis)
    pairs = [(i, i + step) for i in range(count) if 0 <= i + step < count]
    return lax.ppermute(value, axis, pairs)


def swap(value, first):
    count = lax.axis_size("across")
    pairs = []
    for i in range(first, count - 1, 2):
        pairs += [(i, i + 1), (i + 1, i)]
    return lax.ppermute(value, "across", pairs)


def vmem_out(*shapes):
    return [pltpu.VMEM(shape, dtype) for shape, dtype in shapes]


def pack_kernel(
    toa_in, seed_in, valid_in, cloud_in, land_in, row_in, col_in,
    go_down, go_up, outer, inner, cells, toa, row_taps, col_taps,
    seed, valid, cloud, land, spot, sems,
):
    moves = [
        (seed_in, seed),
        (valid_in, valid),
        (cloud_in, cloud),
        (land_in, land),
        (toa_in, toa),
        (row_in, row_taps),
        (col_in, col_taps),
    ]
    copies = [pltpu.make_async_copy(x, y, sems.at[i]) for i, (x, y) in enumerate(moves)]
    for copy in copies:
        copy.start()
    for copy in copies[:4]:
        copy.wait()
    core = lax.rem(lax.axis_index("across"), 2)
    sub = iota((8, 128), 0)
    lane = iota((8, 128), 1)
    lane_at = iota((16, 128), 1)
    row_at = iota((16, 128), 0)
    whole = seed[...]
    high = whole.astype(BF16).astype(F32)
    rest = whole - high
    middle = rest.astype(BF16).astype(F32)
    conf = (valid[...] * (1 - cloud[...])).astype(F32)
    values = [high, middle, rest - middle, conf, land[...].astype(F32)]
    copies[4].wait()
    go_down[...] = toa[:, ROWS - HALO :, :]
    go_up[...] = toa[:, :HALO, :]

    def side(ref, offset):
        ref[...] = toa[:, :, offset : offset + SIDE]

    @pl.when(core == 0)
    def _():
        side(outer, 0)
        side(inner, SIDE)

    @pl.when(core == 1)
    def _():
        side(outer, SIDE)
        side(inner, 0)

    spot[...] = jnp.zeros_like(spot)
    blank = jnp.zeros((8, 128), F32)
    for v in range(5):
        spot[0:CELL_ROWS, 4 : 4 + CELL_COLS] = values[v]
        base = spot[...]
        wide = jnp.where(
            lane < 4,
            pltpu.roll(base, 120, 1),
            jnp.where(lane < 12, base, jnp.where(lane < 16, pltpu.roll(base, 8, 1), 0.0)),
        )
        turned = pltpu.roll(wide, 6, 0)
        head = jnp.where(sub < 4, turned, 0.0)
        tile = jnp.concatenate([jnp.where(sub >= 6, turned, 0.0), head], axis=0)
        cells[v] = tile
        first = jnp.concatenate([head, blank], axis=0).astype(BF16)
        last = jnp.concatenate([blank, pltpu.roll(wide, 4, 0)], axis=0).astype(BF16)
        for at in (0, 128):
            go_down[v, 0:16, at : at + 128] = jnp.where(
                row_at < HALO - KR, first, toa[v, ROWS - HALO : ROWS - HALO + 16, at : at + 128]
            )
            go_up[v, HALO - 16 : HALO, at : at + 128] = jnp.where(
                row_at >= 16 - (HALO - KR), last, toa[v, HALO - 16 : HALO, at : at + 128]
            )
        to_right = jnp.where(lane_at < SIDE - KR, tile.astype(BF16), toa[v, 0:16, SIDE:])
        to_left = jnp.where(
            lane_at < KR, toa[v, 0:16, 0:SIDE], pltpu.roll(tile, 112, 1).astype(BF16)
        )
        outer[v, 0:16, :] = jnp.where(core == 0, to_left, to_right)
        inner[v, 0:16, :] = jnp.where(core == 0, to_right, to_left)
    copies[5].wait()
    copies[6].wait()


def pack(toa, seed, valid, cloud, land, row_taps, col_taps):
    cell = (CELL_ROWS, CELL_COLS)
    return pl.pallas_call(
        pack_kernel,
        in_specs=[pl.BlockSpec(memory_space=pltpu.HBM)] * 7,
        out_specs=[VMEM] * 8,
        out_shape=vmem_out(
            ((BANDS, HALO, COLS), BF16),
            ((BANDS, HALO, COLS), BF16),
            ((BANDS, ROWS, SIDE), BF16),
            ((BANDS, ROWS, SIDE), BF16),
            ((5, 16, 128), F32),
            ((BANDS, ROWS, COLS), BF16),
            ((BANDS, 3, TAPS), F32),
            ((BANDS, 3, TAPS), F32),
        ),
        scratch_shapes=[
            pltpu.VMEM(cell, F32),
            pltpu.VMEM(cell, jnp.int32),
            pltpu.VMEM(cell, jnp.int32),
            pltpu.VMEM(cell, jnp.int32),
            pltpu.VMEM((8, 128), F32),
            pltpu.SemaphoreType.DMA((7,)),
        ],
        compiler_params=pltpu.CompilerParams(vmem_limit_bytes=58 << 20),
        name="pack",
    )(toa, seed, valid, cloud, land, row_taps, col_taps)


def toeplitz_kernel(row_ref, col_ref, near_out, far_out, col_out, pad_ref):
    pad_ref[...] = jnp.zeros_like(pad_ref)
    flip = (iota((256, 256), 0) + iota((256, 256), 1) == TAPS + 7).astype(F32).astype(BF16)
    col_index = iota((384, 128), 1) - iota((384, 128), 0) + (SIDE + KR)
    col_good = (col_index >= 0) & (col_index < TAPS)
    row_at = iota((ROWS, 256), 1)
    row_base = row_at - iota((ROWS, 256), 0)
    near = row_base + KR
    near_good = (near >= 0) & (near < TAPS) & (row_at < ROWS)
    down_good = row_base + (ROWS + KR) < TAPS
    above = row_base - (2 * HALO - KR)
    above_good = (above >= 0) & (above < TAPS) & (row_at < 2 * HALO)

    def spread(vector, first):
        wide = jnp.broadcast_to(vector, (128, 256))
        return pltpu.roll(wide, first, 1, stride=1, stride_axis=0)

    def tall(value):
        swapped = jnp.concatenate([value[0:64, 128:256], value[0:64, 0:128]], axis=1)
        return jnp.concatenate([value, swapped], axis=0)

    def one(band, carry):
        raw = row_ref[band]
        pad_ref[0:3, 4 : 4 + TAPS] = raw / jnp.sum(raw, axis=-1, keepdims=True)
        raw = col_ref[band]
        pad_ref[8:11, 4 : 4 + TAPS] = raw / jnp.sum(raw, axis=-1, keepdims=True)
        taps = pad_ref[...].astype(BF16)
        flipped = jnp.dot(taps, flip, preferred_element_type=F32)
        taps = taps.astype(F32)
        for kern in range(3):
            rolled = spread(flipped[8 + kern : 9 + kern], 24)
            rolled = jnp.concatenate(
                [rolled[:, 0:128], rolled[:, 128:256], rolled[:, 0:128]], axis=0
            )
            tile = jnp.where(col_good, rolled, 0.0).astype(BF16)
            col_out[band, :, kern * 128 : (kern + 1) * 128] = tile
            vector = taps[kern : kern + 1]
            part = slice(kern * ROWS, (kern + 1) * ROWS)
            near_out[band, part, :] = jnp.where(
                near_good, tall(spread(vector, 152)), 0.0
            ).astype(BF16)
            far_out[band, part, :] = jnp.where(
                down_good,
                tall(spread(vector, 216)),
                jnp.where(above_good, tall(spread(vector, HALO)), 0.0),
            ).astype(BF16)
        return carry

    lax.fori_loop(0, BANDS, one, 0)


def toeplitz(row_taps, col_taps):
    return pl.pallas_call(
        toeplitz_kernel,
        in_specs=[VMEM] * 2,
        out_specs=[VMEM] * 3,
        out_shape=vmem_out(
            ((BANDS, 3 * ROWS, 256), BF16),
            ((BANDS, 3 * ROWS, 256), BF16),
            ((BANDS, 384, 384), BF16),
        ),
        scratch_shapes=[pltpu.VMEM((16, 256), F32)],
        cost_estimate=pl.CostEstimate(flops=0, bytes_accessed=8_000_000, transcendentals=0),
        compiler_params=pltpu.CompilerParams(vmem_limit_bytes=8 << 20),
        name="toeplitz",
    )(row_taps, col_taps)


def split_kernel(toa, up, down, pace, outer, inner, field):
    del pace
    core = lax.rem(lax.axis_index("across"), 2)

    def fill(left, right):
        left[:, 0:HALO] = down[:, :, 0:SIDE]
        left[:, HALO:] = up[:, :, 0:SIDE]
        right[:, 0:HALO] = down[:, :, SIDE:]
        right[:, HALO:] = up[:, :, SIDE:]

    @pl.when(core == 0)
    def _():
        fill(outer, inner)

    @pl.when(core == 1)
    def _():
        fill(inner, outer)

    field[:, 0:ROWS] = toa[...]
    field[:, ROWS : ROWS + HALO] = down[...]
    field[:, ROWS + HALO :] = up[...]


def split(toa, up, down, pace):
    shape = ((BANDS, 2 * HALO, SIDE), BF16)
    return pl.pallas_call(
        split_kernel,
        in_specs=[VMEM] * 4,
        out_specs=[VMEM] * 3,
        out_shape=vmem_out(shape, shape, ((BANDS, ROWS + 2 * HALO, COLS), BF16)),
        compiler_params=pltpu.CompilerParams(vmem_limit_bytes=4 << 20),
        name="split",
    )(toa, up, down, pace)


def middle_matrix(col_mat, band, kern):
    at = slice(kern * 128, (kern + 1) * 128)
    return jnp.concatenate([col_mat[band, 128:384, at], col_mat[band, 0:256, at]], axis=1)


def side_matrix(col_mat, band, kern):
    at = slice(kern * 128, (kern + 1) * 128)
    blank = jnp.zeros((128, 128), BF16)
    return jnp.concatenate(
        [
            jnp.concatenate([col_mat[band, 0:128, at], blank], axis=1),
            jnp.concatenate([blank, col_mat[band, 256:384, at]], axis=1),
        ],
        axis=0,
    )


def own_kernel(field, outer, inner, near_mat, col_mat, env, halo, passed):
    core = lax.rem(lax.axis_index("across"), 2)
    passed[ROWS:256, :] = jnp.zeros((256 - ROWS, 3 * COLS), BF16)

    def one(band, carry):
        first = outer[band]
        second = inner[band]
        sides = jnp.concatenate(
            [jnp.where(core == 0, first, second), jnp.where(core == 0, second, first)], axis=1
        )
        for kern in range(3):
            at = slice(kern * COLS, (kern + 1) * COLS)
            middle = middle_matrix(col_mat, band, kern)
            value = jnp.dot(field[band], middle, preferred_element_type=F32)
            halo[band, :, at] = value[ROWS:]
            value = value[0:ROWS] + jnp.dot(
                sides, side_matrix(col_mat, band, kern), preferred_element_type=F32
            )
            passed[0:ROWS, at] = value.astype(BF16)
        for kern in range(3):
            at = slice(kern * COLS, (kern + 1) * COLS)
            env[band, :, at] = jnp.dot(
                near_mat[band, kern * ROWS : (kern + 1) * ROWS, :],
                passed[:, at],
                preferred_element_type=F32,
            )
        return carry

    lax.fori_loop(0, BANDS, one, 0, unroll=UNROLL_OWN)


def own_part(field, outer, inner, near_mat, col_mat):
    flops = BANDS * 2 * (192 * 512 * 768 + 208 * 256 * 768 + 192 * 256 * 768)
    return pl.pallas_call(
        own_kernel,
        in_specs=[VMEM] * 5,
        out_specs=[VMEM] * 2,
        out_shape=vmem_out(
            ((BANDS, ROWS, 3 * COLS), F32), ((BANDS, 2 * HALO, 3 * COLS), F32)
        ),
        scratch_shapes=[pltpu.VMEM((256, 3 * COLS), BF16)],
        cost_estimate=pl.CostEstimate(
            flops=flops, bytes_accessed=10_000_000, transcendentals=0
        ),
        compiler_params=pltpu.CompilerParams(vmem_limit_bytes=8 << 20),
        name="own_part",
    )(field, outer, inner, near_mat, col_mat)


def cell_state(core, cells, up, down, outer, inner, far_outer, far_inner):
    sub = iota((8, 128), 0)
    lane = iota((8, 128), 1)
    both = iota((16, 128), 1)
    parts = []
    for v in range(5):
        out_up = far_outer[v, HALO : HALO + 8, :].astype(F32)
        in_up = far_inner[v, HALO : HALO + 8, :].astype(F32)
        out_down = far_outer[v, HALO - 8 : HALO, :].astype(F32)
        in_down = far_inner[v, HALO - 8 : HALO, :].astype(F32)
        out_side = outer[v, 0:16, :].astype(F32)
        in_side = inner[v, 0:16, :].astype(F32)
        top = jnp.where(
            lane < 4,
            jnp.where(core == 0, out_up, in_up),
            jnp.where(lane < 12, up[v, 0:8, 0:128].astype(F32), jnp.where(core == 0, in_up, out_up)),
        )
        low = jnp.where(
            lane < 4,
            jnp.where(core == 0, out_down, in_down),
            jnp.where(
                lane < 12,
                down[v, HALO - 8 : HALO, 0:128].astype(F32),
                jnp.where(core == 0, in_down, out_down),
            ),
        )
        west = jnp.where(core == 0, out_side, in_side)
        east = pltpu.roll(jnp.where(core == 0, in_side, out_side), 16, 1)
        middle = jnp.where(both < 4, west, jnp.where(both < 12, cells[v], east))
        first = jnp.where(sub < 6, pltpu.roll(top, 2, 0), middle[0:8])
        second = jnp.where(sub < 4, middle[8:16], low)
        parts.append(jnp.concatenate([first, second], axis=0))
    seed = parts[0] + parts[1] + parts[2]
    conf = parts[3]
    kind = parts[4]
    prior = jnp.where(kind < 0.5, 0.06, jnp.where(kind < 1.5, 0.2, 0.45))
    row = lax.axis_index("along") * CELL_ROWS + iota((16, 128), 0) - 6
    col = lax.axis_index("across") * CELL_COLS + iota((16, 128), 1) - 4
    last_row = lax.axis_size("along") * CELL_ROWS - 1
    last_col = lax.axis_size("across") * CELL_COLS - 1
    inside = (row >= 0) & (row <= last_row) & (col >= 0) & (col <= last_col)
    count = (
        (row > 0).astype(F32)
        + (row < last_row).astype(F32)
        + (col > 0).astype(F32)
        + (col < last_col).astype(F32)
    )
    count = jnp.maximum(count, 1.0)
    fix = conf * seed + (1.0 - conf) * (0.3 * prior)
    mult = 0.7 * (1.0 - conf)
    aot = jnp.where(inside, conf * seed + (1.0 - conf) * prior, 0.0)
    for _ in range(SWEEPS):
        near = (
            pltpu.roll(aot, 15, 0)
            + pltpu.roll(aot, 1, 0)
            + pltpu.roll(aot, 127, 1)
            + pltpu.roll(aot, 1, 1)
        )
        aot = jnp.where(inside, fix + mult * (near / count), 0.0)
    return pltpu.roll(aot, 10, 0)[0:8]


def last_kernel(
    tau, adjacency, toa, up, down, outer, inner, cells, far_outer, far_inner,
    far_mat, col_mat, env, halo, out, passed, fine, result, sems,
):
    core = lax.rem(lax.axis_index("across"), 2)
    small = cell_state(core, cells, up, down, outer, inner, far_outer, far_inner)
    block = iota((8, COLS), 1) // CB
    aot = jnp.zeros((8, COLS), F32)
    for j in range(CELL_COLS):
        aot = jnp.where(block == j, small[:, 4 + j : 5 + j], aot)
    gauss = []
    for center in (0.1, 0.35, 0.7):
        offset = aot - center
        gauss.append(jnp.exp(-(offset * offset) / 0.08))
    total = gauss[0] + gauss[1] + gauss[2]
    fine[0:8, :] = aot
    for kern in range(3):
        fine[8 + 8 * kern : 16 + 8 * kern, :] = gauss[kern] / total
    passed[2 * HALO : 256, :] = jnp.zeros((256 - 2 * HALO, 3 * COLS), BF16)

    def copy(band):
        return pltpu.make_async_copy(result.at[band], out.at[band], sems.at[band])

    def one(band, carry):
        first = far_outer[band]
        second = far_inner[band]
        sides = jnp.concatenate(
            [jnp.where(core == 0, first, second), jnp.where(core == 0, second, first)], axis=1
        )
        for kern in range(3):
            at = slice(kern * COLS, (kern + 1) * COLS)
            value = jnp.dot(
                sides, side_matrix(col_mat, band, kern), preferred_element_type=F32
            )
            passed[0 : 2 * HALO, at] = (value + halo[band, :, at]).astype(BF16)
        growth = jnp.exp(tau[band] * fine[0:8, :])
        own = (1.0 + adjacency[band]) * growth
        scaled = adjacency[band] * growth
        sums = [
            env[band, :, kern * COLS : (kern + 1) * COLS]
            + jnp.dot(
                far_mat[band, kern * ROWS : (kern + 1) * ROWS, :],
                passed[:, kern * COLS : (kern + 1) * COLS],
                preferred_element_type=F32,
            )
            for kern in range(3)
        ]
        weights = [scaled * fine[8 + 8 * kern : 16 + 8 * kern, :] for kern in range(3)]
        for i in range(CELL_ROWS):
            part = slice(i * CB, (i + 1) * CB)
            value = own[i : i + 1, :] * toa[band, part, :].astype(F32)
            for kern in range(3):
                value = value - weights[kern][i : i + 1, :] * sums[kern][part, :]
            result[band, part, :] = value
        copy(band).start()
        return carry

    lax.fori_loop(0, BANDS, one, 0, unroll=UNROLL_LAST)
    for band in range(BANDS):
        copy(band).wait()


def last_part(tau, adjacency, toa, up, down, outer, inner, cells, far_outer, far_inner, far_mat, col_mat, env, halo):
    flops = BANDS * 2 * (208 * 256 * 768 + 192 * 256 * 768)
    return pl.pallas_call(
        last_kernel,
        in_specs=[SMEM, SMEM] + [VMEM] * 12,
        out_specs=pl.BlockSpec(memory_space=pl.ANY),
        out_shape=jax.ShapeDtypeStruct((BANDS, ROWS, COLS), F32),
        scratch_shapes=[
            pltpu.VMEM((256, 3 * COLS), BF16),
            pltpu.VMEM((32, COLS), F32),
            pltpu.VMEM((BANDS, ROWS, COLS), F32),
            pltpu.SemaphoreType.DMA((BANDS,)),
        ],
        cost_estimate=pl.CostEstimate(
            flops=flops, bytes_accessed=12_000_000, transcendentals=0
        ),
        compiler_params=pltpu.CompilerParams(vmem_limit_bytes=8 << 20),
        name="last_part",
    )(
        tau, adjacency, toa, up, down, outer, inner, cells, far_outer, far_inner,
        far_mat, col_mat, env, halo,
    )


def body(toa, aot_seed, valid, cloud, land_class, row_taps, col_taps, tau, adjacency):
    go_down, go_up, to_outer, to_inner, cells, toa, row_taps, col_taps = pack(
        toa, aot_seed, valid, cloud, land_class, row_taps, col_taps
    )
    up = shift(go_down, "along", 1)
    down = shift(go_up, "along", -1)
    outer = swap(to_outer, 1)
    inner = swap(to_inner, 0)
    near_mat, far_mat, col_mat = toeplitz(row_taps, col_taps)
    far_to_outer, far_to_inner, field = split(toa, up, down, near_mat)
    far_outer = swap(far_to_outer, 1)
    far_inner = swap(far_to_inner, 0)
    env, halo = own_part(field, outer, inner, near_mat, col_mat)
    return last_part(
        tau, adjacency, toa, up, down, outer, inner, cells, far_outer, far_inner,
        far_mat, col_mat, env, halo,
    )


def solution(mesh):
    cells = P("along", "across")
    in_specs = (P(None, "along", "across"), cells, cells, cells, cells, P(), P(), P(), P())
    out_specs = P(None, "along", "across")
    return jax.shard_map(body, mesh=mesh, in_specs=in_specs, out_specs=out_specs, check_vma=False)
```

profile of v0, /device:TPU:102, one launch (start us, length us, event | category | flops | bytes accessed | tf_op | source)
XLA Modules:
  0.0 32.7 jit_solution(17488531404909651439)
XLA Ops:
  0.0 1.6 %pack.1 = (bf16[6,104,256]{2,1,0:T(8,128)(2,1)S(1)}, bf16[6,104,256]{2,1,0:T(8,128)(2,1)S(1)}, bf16[6,192,128]{2,1,0:T(8,128)(2,1)S(1)}, bf16[6,192,128]{2,1,0:T...) custom-call(bf16[6,192,256]{2,1,0:T(8,128)(2,1)} %toa_in.1, ...), custom_call_target="tpu_custom_call" | custom-call | tf_op jit(solution)/shard_map/pack/pallas_call | solution.py:131
  1.6 5.0 %collective-permute-start = (bf16[6,104,256]{2,1,0:T(8,128)(2,1)S(1)}, bf16[6,104,256]{2,1,0:T(8,128)(2,1)S(1)}, u32[]{:S(2)}, u32[]{:S(2)}) collective-permute-start(bf16[6,104,256]{2,1,0:T(8,128)(2,1)S(1)} %get-tuple-element.22), channel_id=1, source_target_pairs={{0,32},{32,64},{64,96},{96,128},{128,160},{160,192},{192,224},{224... | collective-permute-start | bytes 958472 | tf_op jit(solution)/shard_map/ppermute | solution.py:34
  6.6 1.9 %collective-permute-start.1 = (bf16[6,104,256]{2,1,0:T(8,128)(2,1)S(1)}, bf16[6,104,256]{2,1,0:T(8,128)(2,1)S(1)}, u32[]{:S(2)}, u32[]{:S(2)}) collective-permute-start(bf16[6,104,256]{2,1,0:T(8,128)(2,1)S(1)} %get-tuple-element.23), channel_id=1, source_target_pairs={{32,0},{64,32},{96,64},{128,96},{160,128},{192,160},{224,192},{256... | collective-permute-start | bytes 958472 | tf_op jit(solution)/shard_map/ppermute | solution.py:34
  8.6 4.3 %collective-permute-start.2 = (bf16[6,192,128]{2,1,0:T(8,128)(2,1)S(1)}, bf16[6,192,128]{2,1,0:T(8,128)(2,1)S(1)}, u32[]{:S(2)}, u32[]{:S(2)}) collective-permute-start(bf16[6,192,128]{2,1,0:T(8,128)(2,1)S(1)} %get-tuple-element.24), channel_id=1, source_target_pairs={{1,2},{2,1},{3,4},{4,3},{5,6},{6,5},{7,8},{8,7},{9,10},{10,9},{11,... | collective-permute-start | bytes 884744 | tf_op jit(solution)/shard_map/ppermute | solution.py:42
  12.9 1.9 %collective-permute-start.3 = (bf16[6,192,128]{2,1,0:T(8,128)(2,1)S(1)}, bf16[6,192,128]{2,1,0:T(8,128)(2,1)S(1)}, u32[]{:S(2)}, u32[]{:S(2)}) collective-permute-start(bf16[6,192,128]{2,1,0:T(8,128)(2,1)S(1)} %get-tuple-element.25), channel_id=1, source_target_pairs={{0,1},{1,0},{2,3},{3,2},{4,5},{5,4},{6,7},{7,6},{8,9},{9,8},{10,11... | collective-permute-start | bytes 884744 | tf_op jit(solution)/shard_map/ppermute | solution.py:42
  14.8 3.0 %toeplitz.1 = (bf16[6,576,256]{2,1,0:T(8,128)(2,1)S(1)}, bf16[6,576,256]{2,1,0:T(8,128)(2,1)S(1)}, bf16[6,384,384]{2,1,0:T(8,128)(2,1)S(1)}) custom-call(f32[6,3,201]{2,1,0:T(4,128)S(1)} %get-tuple-element.27.row_ref, f32[6,3,201]{2,1,0:T(4,128)S(1)} %get-tuple-element.28.col_ref), custom_call_target="tpu_custom_call" | custom-call | bytes 8000000 | tf_op jit(solution)/shard_map/toeplitz/pallas_call | solution.py:210
  17.8 0.0 collective-permute-done.up
  17.8 0.9 %collective-permute-done.1.down = bf16[6,104,256]{2,1,0:T(8,128)(2,1)S(1)} collective-permute-done((bf16[6,104,256]{2,1,0:T(8,128)(2,1)S(1)}, bf16[6,104,256]{2,1,0:T(8,128)(2,1)S(1)}, u32[]{:S(2)}, u32[]{:S(2)}) %collective-permute-start.1) | collective-permute-done | bytes 319520 | tf_op jit(solution)/shard_map/ppermute | solution.py:34
  18.7 0.2 split.1
  18.9 3.4 %collective-permute-start.4 = (bf16[6,208,128]{2,1,0:T(8,128)(2,1)S(1)}, bf16[6,208,128]{2,1,0:T(8,128)(2,1)S(1)}, u32[]{:S(2)}, u32[]{:S(2)}) collective-permute-start(bf16[6,208,128]{2,1,0:T(8,128)(2,1)S(1)} %get-tuple-element.30), channel_id=1, source_target_pairs={{1,2},{2,1},{3,4},{4,3},{5,6},{6,5},{7,8},{8,7},{9,10},{10,9},{11,... | collective-permute-start | bytes 958472 | tf_op jit(solution)/shard_map/ppermute | solution.py:42
  22.4 2.1 %collective-permute-start.5 = (bf16[6,208,128]{2,1,0:T(8,128)(2,1)S(1)}, bf16[6,208,128]{2,1,0:T(8,128)(2,1)S(1)}, u32[]{:S(2)}, u32[]{:S(2)}) collective-permute-start(bf16[6,208,128]{2,1,0:T(8,128)(2,1)S(1)} %get-tuple-element.31), channel_id=1, source_target_pairs={{0,1},{1,0},{2,3},{3,2},{4,5},{5,4},{6,7},{7,6},{8,9},{9,8},{10,11... | collective-permute-start | bytes 958472 | tf_op jit(solution)/shard_map/ppermute | solution.py:42
  24.5 0.0 collective-permute-done.2.outer
  24.5 0.0 collective-permute-done.3.inner
  24.5 0.0 copy-start
  24.5 0.0 copy-start.1
  24.5 4.0 %own_part.1 = (f32[6,192,768]{2,1,0:T(8,128)S(1)}, f32[6,208,768]{2,1,0:T(8,128)S(1)}) custom-call(bf16[6,400,256]{2,1,0:T(8,128)(2,1)S(1)} %get-tuple-element.34.field, bf16[6,192,128]{2,1,0:T(8,128)(2,1)S(1)} %collective-permute-done.2.outer, bf16[6,192,128]{2,1,0:T(8,128)(2,1)S(1)} %collective-permute-done.3.inner, ...), custom_call_target="tpu_custom_call" | custom-call | flops 1849688064 | bytes 10000000 | tf_op jit(solution)/shard_map/own_part/pallas_call | solution.py:311
  28.5 0.9 %collective-permute-done.4.far_outer = bf16[6,208,128]{2,1,0:T(8,128)(2,1)S(1)} collective-permute-done((bf16[6,208,128]{2,1,0:T(8,128)(2,1)S(1)}, bf16[6,208,128]{2,1,0:T(8,128)(2,1)S(1)}, u32[]{:S(2)}, u32[]{:S(2)}) %collective-permute-start.4) | collective-permute-done | bytes 319520 | tf_op jit(solution)/shard_map/ppermute | solution.py:42
  29.3 0.0 collective-permute-done.5.far_inner
  29.3 0.0 copy-done
  29.4 0.0 copy-done.1
  29.4 3.4 %last_part.1 = f32[6,192,256]{2,1,0:T(8,128)} custom-call(f32[6]{0:T(128)S(1)} %copy-done, f32[6]{0:T(128)S(1)} %copy-done.1, bf16[6,192,256]{2,1,0:T(8,128)(2,1)S(1)} %get-tuple-element.21.toa, bf16[6,104,256]{2,1,0:T(8,128)(2,1)S(1)} %collective-permute-done.up, bf16[6,104,256]{2,1,0:T(8,128)(2,1)S(1)} %collective-permute-done.1.down, ...), custom_call_target="tpu_custom_call" | custom-call | flops 943718400 | bytes 12000000 | tf_op jit(solution)/shard_map/last_part/pallas_call | solution.py:453
Async XLA Ops:
  1.6 16.3 %collective-permute-start = (bf16[6,104,256]{2,1,0:T(8,128)(2,1)S(1)}, bf16[6,104,256]{2,1,0:T(8,128)(2,1)S(1)}, u32[]{:S(2)}, u32[]{:S(2)}) collective-permute-start(bf16[6,104,256]{2,1,0:T(8,128)(2,1)S(1)} %get-tuple-element.22), channel_id=1, source_target_pairs={{0,32},{32,64},{64,96},{96,128},{128,160},{160,192},{192,224},{224... | collective-permute-start | bytes 958472 | tf_op jit(solution)/shard_map/ppermute | solution.py:34
  6.6 12.1 %collective-permute-start.1 = (bf16[6,104,256]{2,1,0:T(8,128)(2,1)S(1)}, bf16[6,104,256]{2,1,0:T(8,128)(2,1)S(1)}, u32[]{:S(2)}, u32[]{:S(2)}) collective-permute-start(bf16[6,104,256]{2,1,0:T(8,128)(2,1)S(1)} %get-tuple-element.23), channel_id=1, source_target_pairs={{32,0},{64,32},{96,64},{128,96},{160,128},{192,160},{224,192},{256... | collective-permute-start | bytes 958472 | tf_op jit(solution)/shard_map/ppermute | solution.py:34
  8.6 15.9 %collective-permute-start.2 = (bf16[6,192,128]{2,1,0:T(8,128)(2,1)S(1)}, bf16[6,192,128]{2,1,0:T(8,128)(2,1)S(1)}, u32[]{:S(2)}, u32[]{:S(2)}) collective-permute-start(bf16[6,192,128]{2,1,0:T(8,128)(2,1)S(1)} %get-tuple-element.24), channel_id=1, source_target_pairs={{1,2},{2,1},{3,4},{4,3},{5,6},{6,5},{7,8},{8,7},{9,10},{10,9},{11,... | collective-permute-start | bytes 884744 | tf_op jit(solution)/shard_map/ppermute | solution.py:42
  12.9 11.6 %collective-permute-start.3 = (bf16[6,192,128]{2,1,0:T(8,128)(2,1)S(1)}, bf16[6,192,128]{2,1,0:T(8,128)(2,1)S(1)}, u32[]{:S(2)}, u32[]{:S(2)}) collective-permute-start(bf16[6,192,128]{2,1,0:T(8,128)(2,1)S(1)} %get-tuple-element.25), channel_id=1, source_target_pairs={{0,1},{1,0},{2,3},{3,2},{4,5},{5,4},{6,7},{7,6},{8,9},{9,8},{10,11... | collective-permute-start | bytes 884744 | tf_op jit(solution)/shard_map/ppermute | solution.py:42
  18.9 10.4 %collective-permute-start.4 = (bf16[6,208,128]{2,1,0:T(8,128)(2,1)S(1)}, bf16[6,208,128]{2,1,0:T(8,128)(2,1)S(1)}, u32[]{:S(2)}, u32[]{:S(2)}) collective-permute-start(bf16[6,208,128]{2,1,0:T(8,128)(2,1)S(1)} %get-tuple-element.30), channel_id=1, source_target_pairs={{1,2},{2,1},{3,4},{4,3},{5,6},{6,5},{7,8},{8,7},{9,10},{10,9},{11,... | collective-permute-start | bytes 958472 | tf_op jit(solution)/shard_map/ppermute | solution.py:42
  22.4 7.0 %collective-permute-start.5 = (bf16[6,208,128]{2,1,0:T(8,128)(2,1)S(1)}, bf16[6,208,128]{2,1,0:T(8,128)(2,1)S(1)}, u32[]{:S(2)}, u32[]{:S(2)}) collective-permute-start(bf16[6,208,128]{2,1,0:T(8,128)(2,1)S(1)} %get-tuple-element.31), channel_id=1, source_target_pairs={{0,1},{1,0},{2,3},{3,2},{4,5},{5,4},{6,7},{7,6},{8,9},{9,8},{10,11... | collective-permute-start | bytes 958472 | tf_op jit(solution)/shard_map/ppermute | solution.py:42
  24.5 4.9 %copy-start = (f32[6]{0:T(128)S(1)}, f32[6]{0:T(128)}, u32[]{:S(2)}) copy-start(f32[6]{0:T(128)} %tau.1) | copy-start | bytes 76
  24.5 4.9 %copy-start.1 = (f32[6]{0:T(128)S(1)}, f32[6]{0:T(128)}, u32[]{:S(2)}) copy-start(f32[6]{0:T(128)} %adjacency.1) | copy-start | bytes 76
where the time goes:
time: 33 us; the launch traced here: 32.7 us
  starting transfers between devices  18.7 us (57%)
  Pallas kernels  12.1 us (37%)
  waiting for transfers between devices  1.77 us (5%)
    ppermute x4, starting transfers between devices, swap(): return lax.ppermute(value, 'across', pairs)  11.8 us
    ppermute x2, starting transfers between devices, shift(): return lax.ppermute(value, axis, pairs)  6.96 us
    pallas_call x1, Pallas kernels, own_part(): pl.pallas_call(own_kernel, in_specs=[VMEM] * 5, out_specs=[VMEM] * 2, out...  3.97 us
    pallas_call x1, Pallas kernels, last_part(): pl.pallas_call(last_kernel, in_specs=[SMEM, SMEM] + [VMEM] * 12, out_spec...  3.38 us
    pallas_call x1, Pallas kernels, toeplitz(): pl.pallas_call(toeplitz_kernel, in_specs=[VMEM] * 2, out_specs=[VMEM] * 3...  2.98 us
    pallas_call x1, Pallas kernels, pack(): pl.pallas_call(pack_kernel, in_specs=[pl.BlockSpec(memory_space=pltpu.HBM...  1.58 us
    ppermute x2, waiting for transfers between devices, shift(): return lax.ppermute(value, axis, pairs)  0.89 us
    ppermute x4, waiting for transfers between devices, swap(): return lax.ppermute(value, 'across', pairs)  0.88 us
  transfers between devices with their start and end apart: 6, of which 2 were waited for; matrix products, arithmetic and copies ran while one was open for 0% of the time, Pallas kernels for 22%

commit v1 on v0

--- a/solution.py
+++ b/solution.py
@@ -16,8 +16,6 @@
 SIDE = 128
 CELL_ROWS = 6
 CELL_COLS = 8
-UNROLL_OWN = False
-UNROLL_LAST = True
 F32 = jnp.float32
 BF16 = jnp.bfloat16
 VMEM = pl.BlockSpec(memory_space=pltpu.VMEM)
@@ -28,10 +26,16 @@
     return lax.broadcasted_iota(jnp.int32, shape, dim)
 
 
-def shift(value, axis, step):
-    count = lax.axis_size(axis)
-    pairs = [(i, i + step) for i in range(count) if 0 <= i + step < count]
-    return lax.ppermute(value, axis, pairs)
+def exchange(value, step):
+    rows = lax.axis_size("along")
+    cols = lax.axis_size("across")
+    pairs = []
+    for i in range(rows):
+        for j in range(cols):
+            to = i + (step if j % 2 == 0 else -step)
+            if 0 <= to < rows:
+                pairs.append((i * cols + j, to * cols + j))
+    return lax.ppermute(value, ("along", "across"), pairs)
 
 
 def swap(value, first):
@@ -48,7 +52,7 @@
 
 def pack_kernel(
     toa_in, seed_in, valid_in, cloud_in, land_in, row_in, col_in,
-    go_down, go_up, outer, inner, cells, toa, row_taps, col_taps,
+    early, late, outer, inner, cells, toa, row_taps, col_taps,
     seed, valid, cloud, land, spot, sems,
 ):
     moves = [
@@ -76,25 +80,9 @@
     middle = rest.astype(BF16).astype(F32)
     conf = (valid[...] * (1 - cloud[...])).astype(F32)
     values = [high, middle, rest - middle, conf, land[...].astype(F32)]
-    copies[4].wait()
-    go_down[...] = toa[:, ROWS - HALO :, :]
-    go_up[...] = toa[:, :HALO, :]
-
-    def side(ref, offset):
-        ref[...] = toa[:, :, offset : offset + SIDE]
-
-    @pl.when(core == 0)
-    def _():
-        side(outer, 0)
-        side(inner, SIDE)
-
-    @pl.when(core == 1)
-    def _():
-        side(outer, SIDE)
-        side(inner, 0)
-
+    blank = jnp.zeros((8, 128), F32)
     spot[...] = jnp.zeros_like(spot)
-    blank = jnp.zeros((8, 128), F32)
+    tiles = []
     for v in range(5):
         spot[0:CELL_ROWS, 4 : 4 + CELL_COLS] = values[v]
         base = spot[...]
@@ -107,21 +95,45 @@
         head = jnp.where(sub < 4, turned, 0.0)
         tile = jnp.concatenate([jnp.where(sub >= 6, turned, 0.0), head], axis=0)
         cells[v] = tile
-        first = jnp.concatenate([head, blank], axis=0).astype(BF16)
-        last = jnp.concatenate([blank, pltpu.roll(wide, 4, 0)], axis=0).astype(BF16)
-        for at in (0, 128):
-            go_down[v, 0:16, at : at + 128] = jnp.where(
-                row_at < HALO - KR, first, toa[v, ROWS - HALO : ROWS - HALO + 16, at : at + 128]
-            )
-            go_up[v, HALO - 16 : HALO, at : at + 128] = jnp.where(
-                row_at >= 16 - (HALO - KR), last, toa[v, HALO - 16 : HALO, at : at + 128]
-            )
-        to_right = jnp.where(lane_at < SIDE - KR, tile.astype(BF16), toa[v, 0:16, SIDE:])
-        to_left = jnp.where(
-            lane_at < KR, toa[v, 0:16, 0:SIDE], pltpu.roll(tile, 112, 1).astype(BF16)
-        )
-        outer[v, 0:16, :] = jnp.where(core == 0, to_left, to_right)
-        inner[v, 0:16, :] = jnp.where(core == 0, to_right, to_left)
+        tiles.append(
+            (
+                jnp.concatenate([head, blank], axis=0).astype(BF16),
+                jnp.concatenate([blank, pltpu.roll(wide, 4, 0)], axis=0).astype(BF16),
+                tile.astype(BF16),
+                pltpu.roll(tile, 112, 1).astype(BF16),
+            )
+        )
+    copies[4].wait()
+
+    def fill(go_down, go_up, to_left, to_right):
+        go_down[...] = toa[:, ROWS - HALO :, :]
+        go_up[...] = toa[:, :HALO, :]
+        to_left[...] = toa[:, :, :SIDE]
+        to_right[...] = toa[:, :, SIDE:]
+        for v in range(5):
+            first, last, left_cells, right_cells = tiles[v]
+            for at in (0, 128):
+                go_down[v, 0:16, at : at + 128] = jnp.where(
+                    row_at < HALO - KR,
+                    first,
+                    toa[v, ROWS - HALO : ROWS - HALO + 16, at : at + 128],
+                )
+                go_up[v, HALO - 16 : HALO, at : at + 128] = jnp.where(
+                    row_at >= 16 - (HALO - KR), last, toa[v, HALO - 16 : HALO, at : at + 128]
+                )
+            to_right[v, 0:16, :] = jnp.where(
+                lane_at < SIDE - KR, left_cells, toa[v, 0:16, SIDE:]
+            )
+            to_left[v, 0:16, :] = jnp.where(lane_at < KR, toa[v, 0:16, 0:SIDE], right_cells)
+
+    @pl.when(core == 0)
+    def _():
+        fill(early, late, outer, inner)
+
+    @pl.when(core == 1)
+    def _():
+        fill(late, early, inner, outer)
+
     copies[5].wait()
     copies[6].wait()
 
@@ -203,7 +215,7 @@
             ).astype(BF16)
         return carry
 
-    lax.fori_loop(0, BANDS, one, 0)
+    lax.fori_loop(0, BANDS, one, 0, unroll=True)
 
 
 def toeplitz(row_taps, col_taps):
@@ -223,30 +235,30 @@
     )(row_taps, col_taps)
 
 
-def split_kernel(toa, up, down, pace, outer, inner, field):
+def split_kernel(toa, early, late, pace, outer, inner, field):
     del pace
     core = lax.rem(lax.axis_index("across"), 2)
 
-    def fill(left, right):
+    def fill(up, down, left, right):
         left[:, 0:HALO] = down[:, :, 0:SIDE]
         left[:, HALO:] = up[:, :, 0:SIDE]
         right[:, 0:HALO] = down[:, :, SIDE:]
         right[:, HALO:] = up[:, :, SIDE:]
+        field[:, ROWS : ROWS + HALO] = down[...]
+        field[:, ROWS + HALO :] = up[...]
 
     @pl.when(core == 0)
     def _():
-        fill(outer, inner)
+        fill(early, late, outer, inner)
 
     @pl.when(core == 1)
     def _():
-        fill(inner, outer)
+        fill(late, early, inner, outer)
 
     field[:, 0:ROWS] = toa[...]
-    field[:, ROWS : ROWS + HALO] = down[...]
-    field[:, ROWS + HALO :] = up[...]
-
-
-def split(toa, up, down, pace):
+
+
+def split(toa, early, late, pace):
     shape = ((BANDS, 2 * HALO, SIDE), BF16)
     return pl.pallas_call(
         split_kernel,
@@ -255,7 +267,7 @@
         out_shape=vmem_out(shape, shape, ((BANDS, ROWS + 2 * HALO, COLS), BF16)),
         compiler_params=pltpu.CompilerParams(vmem_limit_bytes=4 << 20),
         name="split",
-    )(toa, up, down, pace)
+    )(toa, early, late, pace)
 
 
 def middle_matrix(col_mat, band, kern):
@@ -303,7 +315,7 @@
             )
         return carry
 
-    lax.fori_loop(0, BANDS, one, 0, unroll=UNROLL_OWN)
+    lax.fori_loop(0, BANDS, one, 0, unroll=True)
 
 
 def own_part(field, outer, inner, near_mat, col_mat):
@@ -324,7 +336,8 @@
     )(field, outer, inner, near_mat, col_mat)
 
 
-def cell_state(core, cells, up, down, outer, inner, far_outer, far_inner):
+def cell_state(core, cells, field, outer, inner, far_outer, far_inner):
+    low_at = ROWS + HALO
     sub = iota((8, 128), 0)
     lane = iota((8, 128), 1)
     both = iota((16, 128), 1)
@@ -339,14 +352,14 @@
         top = jnp.where(
             lane < 4,
             jnp.where(core == 0, out_up, in_up),
-            jnp.where(lane < 12, up[v, 0:8, 0:128].astype(F32), jnp.where(core == 0, in_up, out_up)),
+            jnp.where(lane < 12, field[v, low_at : low_at + 8, 0:128].astype(F32), jnp.where(core == 0, in_up, out_up)),
         )
         low = jnp.where(
             lane < 4,
             jnp.where(core == 0, out_down, in_down),
             jnp.where(
                 lane < 12,
-                down[v, HALO - 8 : HALO, 0:128].astype(F32),
+                field[v, low_at - 8 : low_at, 0:128].astype(F32),
                 jnp.where(core == 0, in_down, out_down),
             ),
         )
@@ -387,11 +400,11 @@
 
 
 def last_kernel(
-    tau, adjacency, toa, up, down, outer, inner, cells, far_outer, far_inner,
+    tau, adjacency, field, outer, inner, cells, far_outer, far_inner,
     far_mat, col_mat, env, halo, out, passed, fine, result, sems,
 ):
     core = lax.rem(lax.axis_index("across"), 2)
-    small = cell_state(core, cells, up, down, outer, inner, far_outer, far_inner)
+    small = cell_state(core, cells, field, outer, inner, far_outer, far_inner)
     block = iota((8, COLS), 1) // CB
     aot = jnp.zeros((8, COLS), F32)
     for j in range(CELL_COLS):
@@ -436,23 +449,23 @@
         weights = [scaled * fine[8 + 8 * kern : 16 + 8 * kern, :] for kern in range(3)]
         for i in range(CELL_ROWS):
             part = slice(i * CB, (i + 1) * CB)
-            value = own[i : i + 1, :] * toa[band, part, :].astype(F32)
+            value = own[i : i + 1, :] * field[band, part, :].astype(F32)
             for kern in range(3):
                 value = value - weights[kern][i : i + 1, :] * sums[kern][part, :]
             result[band, part, :] = value
         copy(band).start()
         return carry
 
-    lax.fori_loop(0, BANDS, one, 0, unroll=UNROLL_LAST)
+    lax.fori_loop(0, BANDS, one, 0, unroll=True)
     for band in range(BANDS):
         copy(band).wait()
 
 
-def last_part(tau, adjacency, toa, up, down, outer, inner, cells, far_outer, far_inner, far_mat, col_mat, env, halo):
+def last_part(tau, adjacency, field, outer, inner, cells, far_outer, far_inner, far_mat, col_mat, env, halo):
     flops = BANDS * 2 * (208 * 256 * 768 + 192 * 256 * 768)
     return pl.pallas_call(
         last_kernel,
-        in_specs=[SMEM, SMEM] + [VMEM] * 12,
+        in_specs=[SMEM, SMEM] + [VMEM] * 10,
         out_specs=pl.BlockSpec(memory_space=pl.ANY),
         out_shape=jax.ShapeDtypeStruct((BANDS, ROWS, COLS), F32),
         scratch_shapes=[
@@ -467,26 +480,26 @@
         compiler_params=pltpu.CompilerParams(vmem_limit_bytes=8 << 20),
         name="last_part",
     )(
-        tau, adjacency, toa, up, down, outer, inner, cells, far_outer, far_inner,
+        tau, adjacency, field, outer, inner, cells, far_outer, far_inner,
         far_mat, col_mat, env, halo,
     )
 
 
 def body(toa, aot_seed, valid, cloud, land_class, row_taps, col_taps, tau, adjacency):
-    go_down, go_up, to_outer, to_inner, cells, toa, row_taps, col_taps = pack(
+    to_early, to_late, to_outer, to_inner, cells, toa, row_taps, col_taps = pack(
         toa, aot_seed, valid, cloud, land_class, row_taps, col_taps
     )
-    up = shift(go_down, "along", 1)
-    down = shift(go_up, "along", -1)
+    early = exchange(to_early, 1)
+    late = exchange(to_late, -1)
     outer = swap(to_outer, 1)
     inner = swap(to_inner, 0)
     near_mat, far_mat, col_mat = toeplitz(row_taps, col_taps)
-    far_to_outer, far_to_inner, field = split(toa, up, down, near_mat)
+    far_to_outer, far_to_inner, field = split(toa, early, late, near_mat)
     far_outer = swap(far_to_outer, 1)
     far_inner = swap(far_to_inner, 0)
     env, halo = own_part(field, outer, inner, near_mat, col_mat)
     return last_part(
-        tau, adjacency, toa, up, down, outer, inner, cells, far_outer, far_inner,
+        tau, adjacency, field, outer, inner, cells, far_outer, far_inner,
         far_mat, col_mat, env, halo,
     )
 

time: 33 us -> 31.5 us (0.955)
  Pallas kernels: 12.1 us -> 10.6 us
    ppermute x4, waiting for transfers between devices: 0.88 us -> 1.95 us  [swap(): return lax.ppermute(value, 'across', pairs)]
    ppermute x2, waiting for transfers between devices: 0.89 us -> 0.01 us  [exchange(): return lax.ppermute(value, ('along', 'across'), pairs)]
    pallas_call x1, Pallas kernels: 3.97 us -> 3.16 us  [own_part(): pl.pallas_call(own_kernel, in_specs=[VMEM] * 5, out_specs=[VMEM] * 2, out...]
    pallas_call x1, Pallas kernels: 2.98 us -> 2.56 us  [toeplitz(): pl.pallas_call(toeplitz_kernel, in_specs=[VMEM] * 2, out_specs=[VMEM] * 3...]
  transfers between devices with their start and end apart: 6 -> 6, of which waited for: 2 -> 1; matrix products, arithmetic and copies ran while one was open for 0% -> 0% of each run, Pallas kernels for 22% -> 19%
where the time goes in v1:
time: 31.5 us; the launch traced here: 31.2 us
  starting transfers between devices  18.5 us (59%)
  Pallas kernels  10.6 us (34%)
  waiting for transfers between devices  1.96 us (6%)
    ppermute x4, starting transfers between devices, swap(): return lax.ppermute(value, 'across', pairs)  11.5 us
    ppermute x2, starting transfers between devices, exchange(): return lax.ppermute(value, ('along', 'across'), pairs)  6.96 us
    pallas_call x1, Pallas kernels, last_part(): pl.pallas_call(last_kernel, in_specs=[SMEM, SMEM] + [VMEM] * 10, out_spec...  3.37 us
    pallas_call x1, Pallas kernels, own_part(): pl.pallas_call(own_kernel, in_specs=[VMEM] * 5, out_specs=[VMEM] * 2, out...  3.16 us
    pallas_call x1, Pallas kernels, toeplitz(): pl.pallas_call(toeplitz_kernel, in_specs=[VMEM] * 2, out_specs=[VMEM] * 3...  2.56 us
    ppermute x4, waiting for transfers between devices, swap(): return lax.ppermute(value, 'across', pairs)  1.95 us
    pallas_call x1, Pallas kernels, pack(): pl.pallas_call(pack_kernel, in_specs=[pl.BlockSpec(memory_space=pltpu.HBM...  1.35 us
  transfers between devices with their start and end apart: 6, of which 1 were waited for; matrix products, arithmetic and copies ran while one was open for 0% of the time, Pallas kernels for 19%

profile of v1, /device:TPU:102, one launch (start us, length us, event | category | flops | bytes accessed | tf_op | source)
XLA Modules:
  0.0 31.2 jit_solution(17892186049739782920)
XLA Ops:
  0.0 1.4 %pack.1 = (bf16[6,104,256]{2,1,0:T(8,128)(2,1)S(1)}, bf16[6,104,256]{2,1,0:T(8,128)(2,1)S(1)}, bf16[6,192,128]{2,1,0:T(8,128)(2,1)S(1)}, bf16[6,192,128]{2,1,0:T...) custom-call(bf16[6,192,256]{2,1,0:T(8,128)(2,1)} %toa_in.1, ...), custom_call_target="tpu_custom_call" | custom-call | tf_op jit(solution)/shard_map/pack/pallas_call | solution.py:143
  1.4 5.0 %collective-permute-start = (bf16[6,104,256]{2,1,0:T(8,128)(2,1)S(1)}, bf16[6,104,256]{2,1,0:T(8,128)(2,1)S(1)}, u32[]{:S(2)}, u32[]{:S(2)}) collective-permute-start(bf16[6,104,256]{2,1,0:T(8,128)(2,1)S(1)} %get-tuple-element.22), channel_id=1, source_target_pairs={{0,32},{2,34},{4,36},{6,38},{8,40},{10,42},{12,44},{14,46},{16,48}... | collective-permute-start | bytes 958472 | tf_op jit(solution)/shard_map/ppermute | solution.py:38
  6.4 1.9 %collective-permute-start.1 = (bf16[6,104,256]{2,1,0:T(8,128)(2,1)S(1)}, bf16[6,104,256]{2,1,0:T(8,128)(2,1)S(1)}, u32[]{:S(2)}, u32[]{:S(2)}) collective-permute-start(bf16[6,104,256]{2,1,0:T(8,128)(2,1)S(1)} %get-tuple-element.23), channel_id=1, source_target_pairs={{1,33},{3,35},{5,37},{7,39},{9,41},{11,43},{13,45},{15,47},{17,49}... | collective-permute-start | bytes 958472 | tf_op jit(solution)/shard_map/ppermute | solution.py:38
  8.3 4.3 %collective-permute-start.2 = (bf16[6,192,128]{2,1,0:T(8,128)(2,1)S(1)}, bf16[6,192,128]{2,1,0:T(8,128)(2,1)S(1)}, u32[]{:S(2)}, u32[]{:S(2)}) collective-permute-start(bf16[6,192,128]{2,1,0:T(8,128)(2,1)S(1)} %get-tuple-element.28), channel_id=1, source_target_pairs={{1,2},{2,1},{3,4},{4,3},{5,6},{6,5},{7,8},{8,7},{9,10},{10,9},{11,... | collective-permute-start | bytes 884744 | tf_op jit(solution)/shard_map/ppermute | solution.py:46
  12.7 1.9 %collective-permute-start.3 = (bf16[6,192,128]{2,1,0:T(8,128)(2,1)S(1)}, bf16[6,192,128]{2,1,0:T(8,128)(2,1)S(1)}, u32[]{:S(2)}, u32[]{:S(2)}) collective-permute-start(bf16[6,192,128]{2,1,0:T(8,128)(2,1)S(1)} %get-tuple-element.29), channel_id=1, source_target_pairs={{0,1},{1,0},{2,3},{3,2},{4,5},{5,4},{6,7},{7,6},{8,9},{9,8},{10,11... | collective-permute-start | bytes 884744 | tf_op jit(solution)/shard_map/ppermute | solution.py:46
  14.6 2.6 %toeplitz.1 = (bf16[6,576,256]{2,1,0:T(8,128)(2,1)S(1)}, bf16[6,576,256]{2,1,0:T(8,128)(2,1)S(1)}, bf16[6,384,384]{2,1,0:T(8,128)(2,1)S(1)}) custom-call(f32[6,3,201]{2,1,0:T(4,128)S(1)} %get-tuple-element.24.row_ref, f32[6,3,201]{2,1,0:T(4,128)S(1)} %get-tuple-element.25.col_ref), custom_call_target="tpu_custom_call" | custom-call | bytes 8000000 | tf_op jit(solution)/shard_map/toeplitz/pallas_call | solution.py:222
  17.2 0.0 collective-permute-done.early
  17.2 0.0 collective-permute-done.1.late
  17.2 0.2 split.1
  17.4 3.3 %collective-permute-start.4 = (bf16[6,208,128]{2,1,0:T(8,128)(2,1)S(1)}, bf16[6,208,128]{2,1,0:T(8,128)(2,1)S(1)}, u32[]{:S(2)}, u32[]{:S(2)}) collective-permute-start(bf16[6,208,128]{2,1,0:T(8,128)(2,1)S(1)} %get-tuple-element.31), channel_id=1, source_target_pairs={{1,2},{2,1},{3,4},{4,3},{5,6},{6,5},{7,8},{8,7},{9,10},{10,9},{11,... | collective-permute-start | bytes 958472 | tf_op jit(solution)/shard_map/ppermute | solution.py:46
  20.8 1.9 %collective-permute-start.5 = (bf16[6,208,128]{2,1,0:T(8,128)(2,1)S(1)}, bf16[6,208,128]{2,1,0:T(8,128)(2,1)S(1)}, u32[]{:S(2)}, u32[]{:S(2)}) collective-permute-start(bf16[6,208,128]{2,1,0:T(8,128)(2,1)S(1)} %get-tuple-element.32), channel_id=1, source_target_pairs={{0,1},{1,0},{2,3},{3,2},{4,5},{5,4},{6,7},{7,6},{8,9},{9,8},{10,11... | collective-permute-start | bytes 958472 | tf_op jit(solution)/shard_map/ppermute | solution.py:46
  22.7 0.0 collective-permute-done.2.outer
  22.7 0.0 collective-permute-done.3.inner
  22.7 0.0 copy-start
  22.7 0.0 copy-start.1
  22.7 3.2 %own_part.1 = (f32[6,192,768]{2,1,0:T(8,128)S(1)}, f32[6,208,768]{2,1,0:T(8,128)S(1)}) custom-call(bf16[6,400,256]{2,1,0:T(8,128)(2,1)S(1)} %get-tuple-element.27.field, bf16[6,192,128]{2,1,0:T(8,128)(2,1)S(1)} %collective-permute-done.2.outer, bf16[6,192,128]{2,1,0:T(8,128)(2,1)S(1)} %collective-permute-done.3.inner, ...), custom_call_target="tpu_custom_call" | custom-call | flops 1849688064 | bytes 10000000 | tf_op jit(solution)/shard_map/own_part/pallas_call | solution.py:323
  25.9 1.9 %collective-permute-done.4.far_outer = bf16[6,208,128]{2,1,0:T(8,128)(2,1)S(1)} collective-permute-done((bf16[6,208,128]{2,1,0:T(8,128)(2,1)S(1)}, bf16[6,208,128]{2,1,0:T(8,128)(2,1)S(1)}, u32[]{:S(2)}, u32[]{:S(2)}) %collective-permute-start.4) | collective-permute-done | bytes 319520 | tf_op jit(solution)/shard_map/ppermute | solution.py:46
  27.8 0.0 collective-permute-done.5.far_inner
  27.8 0.0 copy-done
  27.8 0.0 copy-done.1
  27.8 3.4 %last_part.1 = f32[6,192,256]{2,1,0:T(8,128)} custom-call(f32[6]{0:T(128)S(1)} %copy-done, f32[6]{0:T(128)S(1)} %copy-done.1, bf16[6,400,256]{2,1,0:T(8,128)(2,1)S(1)} %get-tuple-element.27.field, bf16[6,192,128]{2,1,0:T(8,128)(2,1)S(1)} %collective-permute-done.2.outer, bf16[6,192,128]{2,1,0:T(8,128)(2,1)S(1)} %collective-permute-done.3.inner, ...), custom_call_target="tpu_custom_call" | custom-call | flops 943718400 | bytes 12000000 | tf_op jit(solution)/shard_map/last_part/pallas_call | solution.py:466
Async XLA Ops:
  1.4 15.8 %collective-permute-start = (bf16[6,104,256]{2,1,0:T(8,128)(2,1)S(1)}, bf16[6,104,256]{2,1,0:T(8,128)(2,1)S(1)}, u32[]{:S(2)}, u32[]{:S(2)}) collective-permute-start(bf16[6,104,256]{2,1,0:T(8,128)(2,1)S(1)} %get-tuple-element.22), channel_id=1, source_target_pairs={{0,32},{2,34},{4,36},{6,38},{8,40},{10,42},{12,44},{14,46},{16,48}... | collective-permute-start | bytes 958472 | tf_op jit(solution)/shard_map/ppermute | solution.py:38
  6.4 10.8 %collective-permute-start.1 = (bf16[6,104,256]{2,1,0:T(8,128)(2,1)S(1)}, bf16[6,104,256]{2,1,0:T(8,128)(2,1)S(1)}, u32[]{:S(2)}, u32[]{:S(2)}) collective-permute-start(bf16[6,104,256]{2,1,0:T(8,128)(2,1)S(1)} %get-tuple-element.23), channel_id=1, source_target_pairs={{1,33},{3,35},{5,37},{7,39},{9,41},{11,43},{13,45},{15,47},{17,49}... | collective-permute-start | bytes 958472 | tf_op jit(solution)/shard_map/ppermute | solution.py:38
  8.3 14.3 %collective-permute-start.2 = (bf16[6,192,128]{2,1,0:T(8,128)(2,1)S(1)}, bf16[6,192,128]{2,1,0:T(8,128)(2,1)S(1)}, u32[]{:S(2)}, u32[]{:S(2)}) collective-permute-start(bf16[6,192,128]{2,1,0:T(8,128)(2,1)S(1)} %get-tuple-element.28), channel_id=1, source_target_pairs={{1,2},{2,1},{3,4},{4,3},{5,6},{6,5},{7,8},{8,7},{9,10},{10,9},{11,... | collective-permute-start | bytes 884744 | tf_op jit(solution)/shard_map/ppermute | solution.py:46
  12.7 10.0 %collective-permute-start.3 = (bf16[6,192,128]{2,1,0:T(8,128)(2,1)S(1)}, bf16[6,192,128]{2,1,0:T(8,128)(2,1)S(1)}, u32[]{:S(2)}, u32[]{:S(2)}) collective-permute-start(bf16[6,192,128]{2,1,0:T(8,128)(2,1)S(1)} %get-tuple-element.29), channel_id=1, source_target_pairs={{0,1},{1,0},{2,3},{3,2},{4,5},{5,4},{6,7},{7,6},{8,9},{9,8},{10,11... | collective-permute-start | bytes 884744 | tf_op jit(solution)/shard_map/ppermute | solution.py:46
  17.4 10.4 %collective-permute-start.4 = (bf16[6,208,128]{2,1,0:T(8,128)(2,1)S(1)}, bf16[6,208,128]{2,1,0:T(8,128)(2,1)S(1)}, u32[]{:S(2)}, u32[]{:S(2)}) collective-permute-start(bf16[6,208,128]{2,1,0:T(8,128)(2,1)S(1)} %get-tuple-element.31), channel_id=1, source_target_pairs={{1,2},{2,1},{3,4},{4,3},{5,6},{6,5},{7,8},{8,7},{9,10},{10,9},{11,... | collective-permute-start | bytes 958472 | tf_op jit(solution)/shard_map/ppermute | solution.py:46
  20.8 7.1 %collective-permute-start.5 = (bf16[6,208,128]{2,1,0:T(8,128)(2,1)S(1)}, bf16[6,208,128]{2,1,0:T(8,128)(2,1)S(1)}, u32[]{:S(2)}, u32[]{:S(2)}) collective-permute-start(bf16[6,208,128]{2,1,0:T(8,128)(2,1)S(1)} %get-tuple-element.32), channel_id=1, source_target_pairs={{0,1},{1,0},{2,3},{3,2},{4,5},{5,4},{6,7},{7,6},{8,9},{9,8},{10,11... | collective-permute-start | bytes 958472 | tf_op jit(solution)/shard_map/ppermute | solution.py:46
  22.7 5.1 %copy-start = (f32[6]{0:T(128)S(1)}, f32[6]{0:T(128)}, u32[]{:S(2)}) copy-start(f32[6]{0:T(128)} %tau.1) | copy-start | bytes 76
  22.7 5.1 %copy-start.1 = (f32[6]{0:T(128)S(1)}, f32[6]{0:T(128)}, u32[]{:S(2)}) copy-start(f32[6]{0:T(128)} %adjacency.1) | copy-start | bytes 76

commit v2 on v1

--- a/solution.py
+++ b/solution.py
@@ -169,7 +169,15 @@
 
 def toeplitz_kernel(row_ref, col_ref, near_out, far_out, col_out, pad_ref):
     pad_ref[...] = jnp.zeros_like(pad_ref)
+    for band in range(BANDS):
+        pad_ref[8 * band : 8 * band + 3, 4 : 4 + TAPS] = row_ref[band]
+        pad_ref[8 * band + 4 : 8 * band + 7, 4 : 4 + TAPS] = col_ref[band]
+    raw = pad_ref[...]
+    total = jnp.sum(raw, axis=-1, keepdims=True)
+    all_taps = (raw / jnp.where(total > 0.0, total, 1.0)).astype(BF16)
     flip = (iota((256, 256), 0) + iota((256, 256), 1) == TAPS + 7).astype(F32).astype(BF16)
+    all_flipped = jnp.dot(all_taps, flip, preferred_element_type=F32)
+    all_taps = all_taps.astype(F32)
     col_index = iota((384, 128), 1) - iota((384, 128), 0) + (SIDE + KR)
     col_good = (col_index >= 0) & (col_index < TAPS)
     row_at = iota((ROWS, 256), 1)
@@ -188,22 +196,16 @@
         swapped = jnp.concatenate([value[0:64, 128:256], value[0:64, 0:128]], axis=1)
         return jnp.concatenate([value, swapped], axis=0)
 
-    def one(band, carry):
-        raw = row_ref[band]
-        pad_ref[0:3, 4 : 4 + TAPS] = raw / jnp.sum(raw, axis=-1, keepdims=True)
-        raw = col_ref[band]
-        pad_ref[8:11, 4 : 4 + TAPS] = raw / jnp.sum(raw, axis=-1, keepdims=True)
-        taps = pad_ref[...].astype(BF16)
-        flipped = jnp.dot(taps, flip, preferred_element_type=F32)
-        taps = taps.astype(F32)
+    for band in range(BANDS):
         for kern in range(3):
-            rolled = spread(flipped[8 + kern : 9 + kern], 24)
+            at = 8 * band + 4 + kern
+            rolled = spread(all_flipped[at : at + 1], 24)
             rolled = jnp.concatenate(
                 [rolled[:, 0:128], rolled[:, 128:256], rolled[:, 0:128]], axis=0
             )
             tile = jnp.where(col_good, rolled, 0.0).astype(BF16)
             col_out[band, :, kern * 128 : (kern + 1) * 128] = tile
-            vector = taps[kern : kern + 1]
+            vector = all_taps[8 * band + kern : 8 * band + kern + 1]
             part = slice(kern * ROWS, (kern + 1) * ROWS)
             near_out[band, part, :] = jnp.where(
                 near_good, tall(spread(vector, 152)), 0.0
@@ -213,9 +215,6 @@
                 tall(spread(vector, 216)),
                 jnp.where(above_good, tall(spread(vector, HALO)), 0.0),
             ).astype(BF16)
-        return carry
-
-    lax.fori_loop(0, BANDS, one, 0, unroll=True)
 
 
 def toeplitz(row_taps, col_taps):
@@ -228,7 +227,7 @@
             ((BANDS, 3 * ROWS, 256), BF16),
             ((BANDS, 384, 384), BF16),
         ),
-        scratch_shapes=[pltpu.VMEM((16, 256), F32)],
+        scratch_shapes=[pltpu.VMEM((8 * BANDS, 256), F32)],
         cost_estimate=pl.CostEstimate(flops=0, bytes_accessed=8_000_000, transcendentals=0),
         compiler_params=pltpu.CompilerParams(vmem_limit_bytes=8 << 20),
         name="toeplitz",
@@ -289,9 +288,10 @@
 
 def own_kernel(field, outer, inner, near_mat, col_mat, env, halo, passed):
     core = lax.rem(lax.axis_index("across"), 2)
-    passed[ROWS:256, :] = jnp.zeros((256 - ROWS, 3 * COLS), BF16)
-
-    def one(band, carry):
+    for slot in range(2):
+        passed[slot, ROWS:256, :] = jnp.zeros((256 - ROWS, 3 * COLS), BF16)
+
+    def columns(band):
         first = outer[band]
         second = inner[band]
         sides = jnp.concatenate(
@@ -305,17 +305,22 @@
             value = value[0:ROWS] + jnp.dot(
                 sides, side_matrix(col_mat, band, kern), preferred_element_type=F32
             )
-            passed[0:ROWS, at] = value.astype(BF16)
+            passed[band % 2, 0:ROWS, at] = value.astype(BF16)
+
+    def rows(band):
         for kern in range(3):
             at = slice(kern * COLS, (kern + 1) * COLS)
             env[band, :, at] = jnp.dot(
                 near_mat[band, kern * ROWS : (kern + 1) * ROWS, :],
-                passed[:, at],
+                passed[band % 2, :, at],
                 preferred_element_type=F32,
             )
-        return carry
-
-    lax.fori_loop(0, BANDS, one, 0, unroll=True)
+
+    columns(0)
+    for band in range(BANDS):
+        if band + 1 < BANDS:
+            columns(band + 1)
+        rows(band)
 
 
 def own_part(field, outer, inner, near_mat, col_mat):
@@ -327,7 +332,7 @@
         out_shape=vmem_out(
             ((BANDS, ROWS, 3 * COLS), F32), ((BANDS, 2 * HALO, 3 * COLS), F32)
         ),
-        scratch_shapes=[pltpu.VMEM((256, 3 * COLS), BF16)],
+        scratch_shapes=[pltpu.VMEM((2, 256, 3 * COLS), BF16)],
         cost_estimate=pl.CostEstimate(
             flops=flops, bytes_accessed=10_000_000, transcendentals=0
         ),
@@ -401,9 +406,26 @@
 
 def last_kernel(
     tau, adjacency, field, outer, inner, cells, far_outer, far_inner,
-    far_mat, col_mat, env, halo, out, passed, fine, result, sems,
+    far_mat, col_mat, env, halo, out, passed, result, sems,
 ):
     core = lax.rem(lax.axis_index("across"), 2)
+    for slot in range(2):
+        passed[slot, 2 * HALO : 256, :] = jnp.zeros((256 - 2 * HALO, 3 * COLS), BF16)
+
+    def columns(band):
+        first = far_outer[band]
+        second = far_inner[band]
+        sides = jnp.concatenate(
+            [jnp.where(core == 0, first, second), jnp.where(core == 0, second, first)], axis=1
+        )
+        for kern in range(3):
+            at = slice(kern * COLS, (kern + 1) * COLS)
+            value = jnp.dot(
+                sides, side_matrix(col_mat, band, kern), preferred_element_type=F32
+            )
+            passed[band % 2, 0 : 2 * HALO, at] = (value + halo[band, :, at]).astype(BF16)
+
+    columns(0)
     small = cell_state(core, cells, field, outer, inner, far_outer, far_inner)
     block = iota((8, COLS), 1) // CB
     aot = jnp.zeros((8, COLS), F32)
@@ -414,49 +436,34 @@
         offset = aot - center
         gauss.append(jnp.exp(-(offset * offset) / 0.08))
     total = gauss[0] + gauss[1] + gauss[2]
-    fine[0:8, :] = aot
-    for kern in range(3):
-        fine[8 + 8 * kern : 16 + 8 * kern, :] = gauss[kern] / total
-    passed[2 * HALO : 256, :] = jnp.zeros((256 - 2 * HALO, 3 * COLS), BF16)
+    weights = [value / total for value in gauss]
 
     def copy(band):
         return pltpu.make_async_copy(result.at[band], out.at[band], sems.at[band])
 
-    def one(band, carry):
-        first = far_outer[band]
-        second = far_inner[band]
-        sides = jnp.concatenate(
-            [jnp.where(core == 0, first, second), jnp.where(core == 0, second, first)], axis=1
-        )
-        for kern in range(3):
-            at = slice(kern * COLS, (kern + 1) * COLS)
-            value = jnp.dot(
-                sides, side_matrix(col_mat, band, kern), preferred_element_type=F32
-            )
-            passed[0 : 2 * HALO, at] = (value + halo[band, :, at]).astype(BF16)
-        growth = jnp.exp(tau[band] * fine[0:8, :])
+    for band in range(BANDS):
+        if band + 1 < BANDS:
+            columns(band + 1)
+        growth = jnp.exp(tau[band] * aot)
         own = (1.0 + adjacency[band]) * growth
         scaled = adjacency[band] * growth
+        factors = [scaled * value for value in weights]
         sums = [
             env[band, :, kern * COLS : (kern + 1) * COLS]
             + jnp.dot(
                 far_mat[band, kern * ROWS : (kern + 1) * ROWS, :],
-                passed[:, kern * COLS : (kern + 1) * COLS],
+                passed[band % 2, :, kern * COLS : (kern + 1) * COLS],
                 preferred_element_type=F32,
             )
             for kern in range(3)
         ]
-        weights = [scaled * fine[8 + 8 * kern : 16 + 8 * kern, :] for kern in range(3)]
         for i in range(CELL_ROWS):
             part = slice(i * CB, (i + 1) * CB)
             value = own[i : i + 1, :] * field[band, part, :].astype(F32)
             for kern in range(3):
-                value = value - weights[kern][i : i + 1, :] * sums[kern][part, :]
+                value = value - factors[kern][i : i + 1, :] * sums[kern][part, :]
             result[band, part, :] = value
         copy(band).start()
-        return carry
-
-    lax.fori_loop(0, BANDS, one, 0, unroll=True)
     for band in range(BANDS):
         copy(band).wait()
 
@@ -469,8 +476,7 @@
         out_specs=pl.BlockSpec(memory_space=pl.ANY),
         out_shape=jax.ShapeDtypeStruct((BANDS, ROWS, COLS), F32),
         scratch_shapes=[
-            pltpu.VMEM((256, 3 * COLS), BF16),
-            pltpu.VMEM((32, COLS), F32),
+            pltpu.VMEM((2, 256, 3 * COLS), BF16),
             pltpu.VMEM((BANDS, ROWS, COLS), F32),
             pltpu.SemaphoreType.DMA((BANDS,)),
         ],

time: 31.5 us -> 30.3 us (0.962)
  the two profiles are of different devices: /device:TPU:102 before, /device:TPU:226 now
where the time goes in v2:
time: 30.3 us; the launch traced here: 30 us
  starting transfers between devices  18.4 us (61%)
  Pallas kernels  7.96 us (26%)
  waiting for transfers between devices  3.49 us (12%)
    ppermute x4, starting transfers between devices, swap(): return lax.ppermute(value, 'across', pairs)  11.5 us
    ppermute x2, starting transfers between devices, exchange(): return lax.ppermute(value, ('along', 'across'), pairs)  6.96 us
    pallas_call x1, Pallas kernels, last_part(): pl.pallas_call(last_kernel, in_specs=[SMEM, SMEM] + [VMEM] * 10, out_spec...  2.89 us
    ppermute x4, waiting for transfers between devices, swap(): return lax.ppermute(value, 'across', pairs)  2.71 us
    pallas_call x1, Pallas kernels, own_part(): pl.pallas_call(own_kernel, in_specs=[VMEM] * 5, out_specs=[VMEM] * 2, out...  2.15 us
    pallas_call x1, Pallas kernels, toeplitz(): pl.pallas_call(toeplitz_kernel, in_specs=[VMEM] * 2, out_specs=[VMEM] * 3...  1.38 us
    pallas_call x1, Pallas kernels, pack(): pl.pallas_call(pack_kernel, in_specs=[pl.BlockSpec(memory_space=pltpu.HBM...  1.35 us
    ppermute x2, waiting for transfers between devices, exchange(): return lax.ppermute(value, ('along', 'across'), pairs)  0.78 us
  transfers between devices with their start and end apart: 6, of which 2 were waited for; matrix products, arithmetic and copies ran while one was open for 0% of the time, Pallas kernels for 12%

profile of v2, /device:TPU:226, one launch (start us, length us, event | category | flops | bytes accessed | tf_op | source)
XLA Modules:
  0.0 30.0 jit_solution(14827794731697799161)
XLA Ops:
  0.0 1.4 %pack.1 = (bf16[6,104,256]{2,1,0:T(8,128)(2,1)S(1)}, bf16[6,104,256]{2,1,0:T(8,128)(2,1)S(1)}, bf16[6,192,128]{2,1,0:T(8,128)(2,1)S(1)}, bf16[6,192,128]{2,1,0:T...) custom-call(bf16[6,192,256]{2,1,0:T(8,128)(2,1)} %toa_in.1, ...), custom_call_target="tpu_custom_call" | custom-call | tf_op jit(solution)/shard_map/pack/pallas_call | solution.py:143
  1.4 5.0 %collective-permute-start = (bf16[6,104,256]{2,1,0:T(8,128)(2,1)S(1)}, bf16[6,104,256]{2,1,0:T(8,128)(2,1)S(1)}, u32[]{:S(2)}, u32[]{:S(2)}) collective-permute-start(bf16[6,104,256]{2,1,0:T(8,128)(2,1)S(1)} %get-tuple-element.22), channel_id=1, source_target_pairs={{0,32},{2,34},{4,36},{6,38},{8,40},{10,42},{12,44},{14,46},{16,48}... | collective-permute-start | bytes 958472 | tf_op jit(solution)/shard_map/ppermute | solution.py:38
  6.4 1.9 %collective-permute-start.1 = (bf16[6,104,256]{2,1,0:T(8,128)(2,1)S(1)}, bf16[6,104,256]{2,1,0:T(8,128)(2,1)S(1)}, u32[]{:S(2)}, u32[]{:S(2)}) collective-permute-start(bf16[6,104,256]{2,1,0:T(8,128)(2,1)S(1)} %get-tuple-element.23), channel_id=1, source_target_pairs={{1,33},{3,35},{5,37},{7,39},{9,41},{11,43},{13,45},{15,47},{17,49}... | collective-permute-start | bytes 958472 | tf_op jit(solution)/shard_map/ppermute | solution.py:38
  8.3 4.1 %collective-permute-start.2 = (bf16[6,192,128]{2,1,0:T(8,128)(2,1)S(1)}, bf16[6,192,128]{2,1,0:T(8,128)(2,1)S(1)}, u32[]{:S(2)}, u32[]{:S(2)}) collective-permute-start(bf16[6,192,128]{2,1,0:T(8,128)(2,1)S(1)} %get-tuple-element.28), channel_id=1, source_target_pairs={{1,2},{2,1},{3,4},{4,3},{5,6},{6,5},{7,8},{8,7},{9,10},{10,9},{11,... | collective-permute-start | bytes 884744 | tf_op jit(solution)/shard_map/ppermute | solution.py:46
  12.4 1.9 %collective-permute-start.3 = (bf16[6,192,128]{2,1,0:T(8,128)(2,1)S(1)}, bf16[6,192,128]{2,1,0:T(8,128)(2,1)S(1)}, u32[]{:S(2)}, u32[]{:S(2)}) collective-permute-start(bf16[6,192,128]{2,1,0:T(8,128)(2,1)S(1)} %get-tuple-element.29), channel_id=1, source_target_pairs={{0,1},{1,0},{2,3},{3,2},{4,5},{5,4},{6,7},{7,6},{8,9},{9,8},{10,11... | collective-permute-start | bytes 884744 | tf_op jit(solution)/shard_map/ppermute | solution.py:46
  14.3 1.4 %toeplitz.1 = (bf16[6,576,256]{2,1,0:T(8,128)(2,1)S(1)}, bf16[6,576,256]{2,1,0:T(8,128)(2,1)S(1)}, bf16[6,384,384]{2,1,0:T(8,128)(2,1)S(1)}) custom-call(f32[6,3,201]{2,1,0:T(4,128)S(1)} %get-tuple-element.24.row_ref, f32[6,3,201]{2,1,0:T(4,128)S(1)} %get-tuple-element.25.col_ref), custom_call_target="tpu_custom_call" | custom-call | bytes 8000000 | tf_op jit(solution)/shard_map/toeplitz/pallas_call | solution.py:221
  15.7 0.0 collective-permute-done.early
  15.7 0.8 %collective-permute-done.1.late = bf16[6,104,256]{2,1,0:T(8,128)(2,1)S(1)} collective-permute-done((bf16[6,104,256]{2,1,0:T(8,128)(2,1)S(1)}, bf16[6,104,256]{2,1,0:T(8,128)(2,1)S(1)}, u32[]{:S(2)}, u32[]{:S(2)}) %collective-permute-start.1) | collective-permute-done | bytes 319520 | tf_op jit(solution)/shard_map/ppermute | solution.py:38
  16.5 0.2 split.1
  16.7 2.9 %collective-permute-start.4 = (bf16[6,208,128]{2,1,0:T(8,128)(2,1)S(1)}, bf16[6,208,128]{2,1,0:T(8,128)(2,1)S(1)}, u32[]{:S(2)}, u32[]{:S(2)}) collective-permute-start(bf16[6,208,128]{2,1,0:T(8,128)(2,1)S(1)} %get-tuple-element.31), channel_id=1, source_target_pairs={{1,2},{2,1},{3,4},{4,3},{5,6},{6,5},{7,8},{8,7},{9,10},{10,9},{11,... | collective-permute-start | bytes 958472 | tf_op jit(solution)/shard_map/ppermute | solution.py:46
  19.6 2.6 %collective-permute-start.5 = (bf16[6,208,128]{2,1,0:T(8,128)(2,1)S(1)}, bf16[6,208,128]{2,1,0:T(8,128)(2,1)S(1)}, u32[]{:S(2)}, u32[]{:S(2)}) collective-permute-start(bf16[6,208,128]{2,1,0:T(8,128)(2,1)S(1)} %get-tuple-element.32), channel_id=1, source_target_pairs={{0,1},{1,0},{2,3},{3,2},{4,5},{5,4},{6,7},{7,6},{8,9},{9,8},{10,11... | collective-permute-start | bytes 958472 | tf_op jit(solution)/shard_map/ppermute | solution.py:46
  22.2 0.0 collective-permute-done.2.outer
  22.2 0.0 collective-permute-done.3.inner
  22.2 0.0 copy-start
  22.3 0.0 copy-start.1
  22.3 2.1 %own_part.1 = (f32[6,192,768]{2,1,0:T(8,128)S(1)}, f32[6,208,768]{2,1,0:T(8,128)S(1)}) custom-call(bf16[6,400,256]{2,1,0:T(8,128)(2,1)S(1)} %get-tuple-element.27.field, bf16[6,192,128]{2,1,0:T(8,128)(2,1)S(1)} %collective-permute-done.2.outer, bf16[6,192,128]{2,1,0:T(8,128)(2,1)S(1)} %collective-permute-done.3.inner, ...), custom_call_target="tpu_custom_call" | custom-call | flops 1849688064 | bytes 10000000 | tf_op jit(solution)/shard_map/own_part/pallas_call | solution.py:328
  24.4 2.7 %collective-permute-done.4.far_outer = bf16[6,208,128]{2,1,0:T(8,128)(2,1)S(1)} collective-permute-done((bf16[6,208,128]{2,1,0:T(8,128)(2,1)S(1)}, bf16[6,208,128]{2,1,0:T(8,128)(2,1)S(1)}, u32[]{:S(2)}, u32[]{:S(2)}) %collective-permute-start.4) | collective-permute-done | bytes 319520 | tf_op jit(solution)/shard_map/ppermute | solution.py:46
  27.1 0.0 collective-permute-done.5.far_inner
  27.1 0.0 copy-done
  27.1 0.0 copy-done.1
  27.1 2.9 %last_part.1 = f32[6,192,256]{2,1,0:T(8,128)} custom-call(f32[6]{0:T(128)S(1)} %copy-done, f32[6]{0:T(128)S(1)} %copy-done.1, bf16[6,400,256]{2,1,0:T(8,128)(2,1)S(1)} %get-tuple-element.27.field, bf16[6,192,128]{2,1,0:T(8,128)(2,1)S(1)} %collective-permute-done.2.outer, bf16[6,192,128]{2,1,0:T(8,128)(2,1)S(1)} %collective-permute-done.3.inner, ...), custom_call_target="tpu_custom_call" | custom-call | flops 943718400 | bytes 12000000 | tf_op jit(solution)/shard_map/last_part/pallas_call | solution.py:473
Async XLA Ops:
  1.4 14.3 %collective-permute-start = (bf16[6,104,256]{2,1,0:T(8,128)(2,1)S(1)}, bf16[6,104,256]{2,1,0:T(8,128)(2,1)S(1)}, u32[]{:S(2)}, u32[]{:S(2)}) collective-permute-start(bf16[6,104,256]{2,1,0:T(8,128)(2,1)S(1)} %get-tuple-element.22), channel_id=1, source_target_pairs={{0,32},{2,34},{4,36},{6,38},{8,40},{10,42},{12,44},{14,46},{16,48}... | collective-permute-start | bytes 958472 | tf_op jit(solution)/shard_map/ppermute | solution.py:38
  6.4 10.1 %collective-permute-start.1 = (bf16[6,104,256]{2,1,0:T(8,128)(2,1)S(1)}, bf16[6,104,256]{2,1,0:T(8,128)(2,1)S(1)}, u32[]{:S(2)}, u32[]{:S(2)}) collective-permute-start(bf16[6,104,256]{2,1,0:T(8,128)(2,1)S(1)} %get-tuple-element.23), channel_id=1, source_target_pairs={{1,33},{3,35},{5,37},{7,39},{9,41},{11,43},{13,45},{15,47},{17,49}... | collective-permute-start | bytes 958472 | tf_op jit(solution)/shard_map/ppermute | solution.py:38
  8.3 13.9 %collective-permute-start.2 = (bf16[6,192,128]{2,1,0:T(8,128)(2,1)S(1)}, bf16[6,192,128]{2,1,0:T(8,128)(2,1)S(1)}, u32[]{:S(2)}, u32[]{:S(2)}) collective-permute-start(bf16[6,192,128]{2,1,0:T(8,128)(2,1)S(1)} %get-tuple-element.28), channel_id=1, source_target_pairs={{1,2},{2,1},{3,4},{4,3},{5,6},{6,5},{7,8},{8,7},{9,10},{10,9},{11,... | collective-permute-start | bytes 884744 | tf_op jit(solution)/shard_map/ppermute | solution.py:46
  12.4 9.8 %collective-permute-start.3 = (bf16[6,192,128]{2,1,0:T(8,128)(2,1)S(1)}, bf16[6,192,128]{2,1,0:T(8,128)(2,1)S(1)}, u32[]{:S(2)}, u32[]{:S(2)}) collective-permute-start(bf16[6,192,128]{2,1,0:T(8,128)(2,1)S(1)} %get-tuple-element.29), channel_id=1, source_target_pairs={{0,1},{1,0},{2,3},{3,2},{4,5},{5,4},{6,7},{7,6},{8,9},{9,8},{10,11... | collective-permute-start | bytes 884744 | tf_op jit(solution)/shard_map/ppermute | solution.py:46
  16.7 10.4 %collective-permute-start.4 = (bf16[6,208,128]{2,1,0:T(8,128)(2,1)S(1)}, bf16[6,208,128]{2,1,0:T(8,128)(2,1)S(1)}, u32[]{:S(2)}, u32[]{:S(2)}) collective-permute-start(bf16[6,208,128]{2,1,0:T(8,128)(2,1)S(1)} %get-tuple-element.31), channel_id=1, source_target_pairs={{1,2},{2,1},{3,4},{4,3},{5,6},{6,5},{7,8},{8,7},{9,10},{10,9},{11,... | collective-permute-start | bytes 958472 | tf_op jit(solution)/shard_map/ppermute | solution.py:46
  19.6 7.5 %collective-permute-start.5 = (bf16[6,208,128]{2,1,0:T(8,128)(2,1)S(1)}, bf16[6,208,128]{2,1,0:T(8,128)(2,1)S(1)}, u32[]{:S(2)}, u32[]{:S(2)}) collective-permute-start(bf16[6,208,128]{2,1,0:T(8,128)(2,1)S(1)} %get-tuple-element.32), channel_id=1, source_target_pairs={{0,1},{1,0},{2,3},{3,2},{4,5},{5,4},{6,7},{7,6},{8,9},{9,8},{10,11... | collective-permute-start | bytes 958472 | tf_op jit(solution)/shard_map/ppermute | solution.py:46
  22.2 4.9 %copy-start = (f32[6]{0:T(128)S(1)}, f32[6]{0:T(128)}, u32[]{:S(2)}) copy-start(f32[6]{0:T(128)} %tau.1) | copy-start | bytes 76
  22.3 4.9 %copy-start.1 = (f32[6]{0:T(128)S(1)}, f32[6]{0:T(128)}, u32[]{:S(2)}) copy-start(f32[6]{0:T(128)} %adjacency.1) | copy-start | bytes 76

commit v3 on v2

--- a/solution.py
+++ b/solution.py
@@ -19,7 +19,6 @@
 F32 = jnp.float32
 BF16 = jnp.bfloat16
 VMEM = pl.BlockSpec(memory_space=pltpu.VMEM)
-SMEM = pl.BlockSpec(memory_space=pltpu.SMEM)
 
 
 def iota(shape, dim):
@@ -32,7 +31,7 @@
     pairs = []
     for i in range(rows):
         for j in range(cols):
-            to = i + (step if j % 2 == 0 else -step)
+            to = i - (step if j % 2 == 0 else -step)
             if 0 <= to < rows:
                 pairs.append((i * cols + j, to * cols + j))
     return lax.ppermute(value, ("along", "across"), pairs)
@@ -51,9 +50,9 @@
 
 
 def pack_kernel(
-    toa_in, seed_in, valid_in, cloud_in, land_in, row_in, col_in,
-    early, late, outer, inner, cells, toa, row_taps, col_taps,
-    seed, valid, cloud, land, spot, sems,
+    toa_in, seed_in, valid_in, cloud_in, land_in, row_in, col_in, tau_in, adjacency_in,
+    early, late, outer, inner, cells, toa, row_taps, col_taps, scales,
+    seed, valid, cloud, land, tau, adjacency, spot, sems,
 ):
     moves = [
         (seed_in, seed),
@@ -63,6 +62,8 @@
         (toa_in, toa),
         (row_in, row_taps),
         (col_in, col_taps),
+        (tau_in, tau),
+        (adjacency_in, adjacency),
     ]
     copies = [pltpu.make_async_copy(x, y, sems.at[i]) for i, (x, y) in enumerate(moves)]
     for copy in copies:
@@ -128,22 +129,25 @@
 
     @pl.when(core == 0)
     def _():
-        fill(early, late, outer, inner)
+        fill(late, early, outer, inner)
 
     @pl.when(core == 1)
     def _():
-        fill(late, early, inner, outer)
-
-    copies[5].wait()
-    copies[6].wait()
-
-
-def pack(toa, seed, valid, cloud, land, row_taps, col_taps):
+        fill(early, late, inner, outer)
+
+    for copy in copies[5:]:
+        copy.wait()
+    for band in range(BANDS):
+        scales[band : band + 1, :] = jnp.full((1, COLS), tau[band], F32)
+        scales[8 + band : 9 + band, :] = jnp.full((1, COLS), adjacency[band], F32)
+
+
+def pack(toa, seed, valid, cloud, land, row_taps, col_taps, tau, adjacency):
     cell = (CELL_ROWS, CELL_COLS)
     return pl.pallas_call(
         pack_kernel,
-        in_specs=[pl.BlockSpec(memory_space=pltpu.HBM)] * 7,
-        out_specs=[VMEM] * 8,
+        in_specs=[pl.BlockSpec(memory_space=pltpu.HBM)] * 9,
+        out_specs=[VMEM] * 9,
         out_shape=vmem_out(
             ((BANDS, HALO, COLS), BF16),
             ((BANDS, HALO, COLS), BF16),
@@ -153,18 +157,21 @@
             ((BANDS, ROWS, COLS), BF16),
             ((BANDS, 3, TAPS), F32),
             ((BANDS, 3, TAPS), F32),
+            ((16, COLS), F32),
         ),
         scratch_shapes=[
             pltpu.VMEM(cell, F32),
             pltpu.VMEM(cell, jnp.int32),
             pltpu.VMEM(cell, jnp.int32),
             pltpu.VMEM(cell, jnp.int32),
+            pltpu.SMEM((BANDS,), F32),
+            pltpu.SMEM((BANDS,), F32),
             pltpu.VMEM((8, 128), F32),
-            pltpu.SemaphoreType.DMA((7,)),
+            pltpu.SemaphoreType.DMA((9,)),
         ],
         compiler_params=pltpu.CompilerParams(vmem_limit_bytes=58 << 20),
         name="pack",
-    )(toa, seed, valid, cloud, land, row_taps, col_taps)
+    )(toa, seed, valid, cloud, land, row_taps, col_taps, tau, adjacency)
 
 
 def toeplitz_kernel(row_ref, col_ref, near_out, far_out, col_out, pad_ref):
@@ -248,11 +255,11 @@
 
     @pl.when(core == 0)
     def _():
-        fill(early, late, outer, inner)
+        fill(late, early, outer, inner)
 
     @pl.when(core == 1)
     def _():
-        fill(late, early, inner, outer)
+        fill(early, late, inner, outer)
 
     field[:, 0:ROWS] = toa[...]
 
@@ -405,7 +412,7 @@
 
 
 def last_kernel(
-    tau, adjacency, field, outer, inner, cells, far_outer, far_inner,
+    scales, field, outer, inner, cells, far_outer, far_inner,
     far_mat, col_mat, env, halo, out, passed, result, sems,
 ):
     core = lax.rem(lax.axis_index("across"), 2)
@@ -444,9 +451,10 @@
     for band in range(BANDS):
         if band + 1 < BANDS:
             columns(band + 1)
-        growth = jnp.exp(tau[band] * aot)
-        own = (1.0 + adjacency[band]) * growth
-        scaled = adjacency[band] * growth
+        growth = jnp.exp(scales[band : band + 1, :] * aot)
+        strength = scales[8 + band : 9 + band, :]
+        own = (1.0 + strength) * growth
+        scaled = strength * growth
         factors = [scaled * value for value in weights]
         sums = [
             env[band, :, kern * COLS : (kern + 1) * COLS]
@@ -468,11 +476,11 @@
         copy(band).wait()
 
 
-def last_part(tau, adjacency, field, outer, inner, cells, far_outer, far_inner, far_mat, col_mat, env, halo):
+def last_part(scales, field, outer, inner, cells, far_outer, far_inner, far_mat, col_mat, env, halo):
     flops = BANDS * 2 * (208 * 256 * 768 + 192 * 256 * 768)
     return pl.pallas_call(
         last_kernel,
-        in_specs=[SMEM, SMEM] + [VMEM] * 10,
+        in_specs=[VMEM] * 11,
         out_specs=pl.BlockSpec(memory_space=pl.ANY),
         out_shape=jax.ShapeDtypeStruct((BANDS, ROWS, COLS), F32),
         scratch_shapes=[
@@ -486,14 +494,14 @@
         compiler_params=pltpu.CompilerParams(vmem_limit_bytes=8 << 20),
         name="last_part",
     )(
-        tau, adjacency, field, outer, inner, cells, far_outer, far_inner,
+        scales, field, outer, inner, cells, far_outer, far_inner,
         far_mat, col_mat, env, halo,
     )
 
 
 def body(toa, aot_seed, valid, cloud, land_class, row_taps, col_taps, tau, adjacency):
-    to_early, to_late, to_outer, to_inner, cells, toa, row_taps, col_taps = pack(
-        toa, aot_seed, valid, cloud, land_class, row_taps, col_taps
+    to_early, to_late, to_outer, to_inner, cells, toa, row_taps, col_taps, scales = pack(
+        toa, aot_seed, valid, cloud, land_class, row_taps, col_taps, tau, adjacency
     )
     early = exchange(to_early, 1)
     late = exchange(to_late, -1)
@@ -505,7 +513,7 @@
     far_inner = swap(far_to_inner, 0)
     env, halo = own_part(field, outer, inner, near_mat, col_mat)
     return last_part(
-        tau, adjacency, field, outer, inner, cells, far_outer, far_inner,
+        scales, field, outer, inner, cells, far_outer, far_inner,
         far_mat, col_mat, env, halo,
     )
 

time: 30.3 us -> 29.3 us (0.967)
  the two profiles are of different devices: /device:TPU:226 before, /device:TPU:102 now
where the time goes in v3:
time: 29.3 us; the launch traced here: 29 us
  starting transfers between devices  18.8 us (64%)
  Pallas kernels  7.45 us (25%)
  waiting for transfers between devices  2.65 us (9%)
    ppermute x4, starting transfers between devices, swap(): return lax.ppermute(value, 'across', pairs)  11.7 us
    ppermute x2, starting transfers between devices, exchange(): return lax.ppermute(value, ('along', 'across'), pairs)  7.05 us
    ppermute x4, waiting for transfers between devices, swap(): return lax.ppermute(value, 'across', pairs)  2.64 us
    pallas_call x1, Pallas kernels, last_part(): pl.pallas_call(last_kernel, in_specs=[VMEM] * 11, out_specs=pl.BlockSpec(...  2.31 us
    pallas_call x1, Pallas kernels, own_part(): pl.pallas_call(own_kernel, in_specs=[VMEM] * 5, out_specs=[VMEM] * 2, out...  2.17 us
    pallas_call x1, Pallas kernels, pack(): pl.pallas_call(pack_kernel, in_specs=[pl.BlockSpec(memory_space=pltpu.HBM...  1.4 us
    pallas_call x1, Pallas kernels, toeplitz(): pl.pallas_call(toeplitz_kernel, in_specs=[VMEM] * 2, out_specs=[VMEM] * 3...  1.38 us
  transfers between devices with their start and end apart: 6, of which 1 were waited for; matrix products, arithmetic and copies ran while one was open for 0% of the time, Pallas kernels for 13%

profile of v3, /device:TPU:102, one launch (start us, length us, event | category | flops | bytes accessed | tf_op | source)
XLA Modules:
  0.0 29.0 jit_solution(2094397869237901070)
XLA Ops:
  0.0 1.4 %pack.1 = (bf16[6,104,256]{2,1,0:T(8,128)(2,1)S(1)}, bf16[6,104,256]{2,1,0:T(8,128)(2,1)S(1)}, bf16[6,192,128]{2,1,0:T(8,128)(2,1)S(1)}, bf16[6,192,128]{2,1,0:T...) custom-call(bf16[6,192,256]{2,1,0:T(8,128)(2,1)} %toa_in.1, ...), custom_call_target="tpu_custom_call" | custom-call | tf_op jit(solution)/shard_map/pack/pallas_call | solution.py:147
  1.4 2.0 %collective-permute-start = (bf16[6,104,256]{2,1,0:T(8,128)(2,1)S(1)}, bf16[6,104,256]{2,1,0:T(8,128)(2,1)S(1)}, u32[]{:S(2)}, u32[]{:S(2)}) collective-permute-start(bf16[6,104,256]{2,1,0:T(8,128)(2,1)S(1)} %get-tuple-element.24), channel_id=1, source_target_pairs={{1,33},{3,35},{5,37},{7,39},{9,41},{11,43},{13,45},{15,47},{17,49}... | collective-permute-start | bytes 958472 | tf_op jit(solution)/shard_map/ppermute | solution.py:37
  3.4 5.0 %collective-permute-start.1 = (bf16[6,104,256]{2,1,0:T(8,128)(2,1)S(1)}, bf16[6,104,256]{2,1,0:T(8,128)(2,1)S(1)}, u32[]{:S(2)}, u32[]{:S(2)}) collective-permute-start(bf16[6,104,256]{2,1,0:T(8,128)(2,1)S(1)} %get-tuple-element.25), channel_id=1, source_target_pairs={{0,32},{2,34},{4,36},{6,38},{8,40},{10,42},{12,44},{14,46},{16,48}... | collective-permute-start | bytes 958472 | tf_op jit(solution)/shard_map/ppermute | solution.py:37
  8.5 4.2 %collective-permute-start.2 = (bf16[6,192,128]{2,1,0:T(8,128)(2,1)S(1)}, bf16[6,192,128]{2,1,0:T(8,128)(2,1)S(1)}, u32[]{:S(2)}, u32[]{:S(2)}) collective-permute-start(bf16[6,192,128]{2,1,0:T(8,128)(2,1)S(1)} %get-tuple-element.30), channel_id=1, source_target_pairs={{1,2},{2,1},{3,4},{4,3},{5,6},{6,5},{7,8},{8,7},{9,10},{10,9},{11,... | collective-permute-start | bytes 884744 | tf_op jit(solution)/shard_map/ppermute | solution.py:45
  12.7 1.9 %collective-permute-start.3 = (bf16[6,192,128]{2,1,0:T(8,128)(2,1)S(1)}, bf16[6,192,128]{2,1,0:T(8,128)(2,1)S(1)}, u32[]{:S(2)}, u32[]{:S(2)}) collective-permute-start(bf16[6,192,128]{2,1,0:T(8,128)(2,1)S(1)} %get-tuple-element.31), channel_id=1, source_target_pairs={{0,1},{1,0},{2,3},{3,2},{4,5},{5,4},{6,7},{7,6},{8,9},{9,8},{10,11... | collective-permute-start | bytes 884744 | tf_op jit(solution)/shard_map/ppermute | solution.py:45
  14.7 1.4 %toeplitz.1 = (bf16[6,576,256]{2,1,0:T(8,128)(2,1)S(1)}, bf16[6,576,256]{2,1,0:T(8,128)(2,1)S(1)}, bf16[6,384,384]{2,1,0:T(8,128)(2,1)S(1)}) custom-call(f32[6,3,201]{2,1,0:T(4,128)S(1)} %get-tuple-element.26.row_ref, f32[6,3,201]{2,1,0:T(4,128)S(1)} %get-tuple-element.27.col_ref), custom_call_target="tpu_custom_call" | custom-call | bytes 8000000 | tf_op jit(solution)/shard_map/toeplitz/pallas_call | solution.py:228
  16.0 0.0 collective-permute-done.early
  16.1 0.0 collective-permute-done.1.late
  16.1 0.2 split.1
  16.3 3.7 %collective-permute-start.4 = (bf16[6,208,128]{2,1,0:T(8,128)(2,1)S(1)}, bf16[6,208,128]{2,1,0:T(8,128)(2,1)S(1)}, u32[]{:S(2)}, u32[]{:S(2)}) collective-permute-start(bf16[6,208,128]{2,1,0:T(8,128)(2,1)S(1)} %get-tuple-element.33), channel_id=1, source_target_pairs={{1,2},{2,1},{3,4},{4,3},{5,6},{6,5},{7,8},{8,7},{9,10},{10,9},{11,... | collective-permute-start | bytes 958472 | tf_op jit(solution)/shard_map/ppermute | solution.py:45
  19.9 1.9 %collective-permute-start.5 = (bf16[6,208,128]{2,1,0:T(8,128)(2,1)S(1)}, bf16[6,208,128]{2,1,0:T(8,128)(2,1)S(1)}, u32[]{:S(2)}, u32[]{:S(2)}) collective-permute-start(bf16[6,208,128]{2,1,0:T(8,128)(2,1)S(1)} %get-tuple-element.34), channel_id=1, source_target_pairs={{0,1},{1,0},{2,3},{3,2},{4,5},{5,4},{6,7},{7,6},{8,9},{9,8},{10,11... | collective-permute-start | bytes 958472 | tf_op jit(solution)/shard_map/ppermute | solution.py:45
  21.9 0.0 collective-permute-done.2.outer
  21.9 0.0 collective-permute-done.3.inner
  21.9 2.2 %own_part.1 = (f32[6,192,768]{2,1,0:T(8,128)S(1)}, f32[6,208,768]{2,1,0:T(8,128)S(1)}) custom-call(bf16[6,400,256]{2,1,0:T(8,128)(2,1)S(1)} %get-tuple-element.29.field, bf16[6,192,128]{2,1,0:T(8,128)(2,1)S(1)} %collective-permute-done.2.outer, bf16[6,192,128]{2,1,0:T(8,128)(2,1)S(1)} %collective-permute-done.3.inner, ...), custom_call_target="tpu_custom_call" | custom-call | flops 1849688064 | bytes 10000000 | tf_op jit(solution)/shard_map/own_part/pallas_call | solution.py:335
  24.1 2.6 %collective-permute-done.4.far_outer = bf16[6,208,128]{2,1,0:T(8,128)(2,1)S(1)} collective-permute-done((bf16[6,208,128]{2,1,0:T(8,128)(2,1)S(1)}, bf16[6,208,128]{2,1,0:T(8,128)(2,1)S(1)}, u32[]{:S(2)}, u32[]{:S(2)}) %collective-permute-start.4) | collective-permute-done | bytes 319520 | tf_op jit(solution)/shard_map/ppermute | solution.py:45
  26.7 0.0 collective-permute-done.5.far_inner
  26.7 2.3 %last_part.1 = f32[6,192,256]{2,1,0:T(8,128)} custom-call(f32[16,256]{1,0:T(8,128)S(1)} %get-tuple-element.22.scales, bf16[6,400,256]{2,1,0:T(8,128)(2,1)S(1)} %get-tuple-element.29.field, bf16[6,192,128]{2,1,0:T(8,128)(2,1)S(1)} %collective-permute-done.2.outer, bf16[6,192,128]{2,1,0:T(8,128)(2,1)S(1)} %collective-permute-done.3.inner, ...), custom_call_target="tpu_custom_call" | custom-call | flops 943718400 | bytes 12000000 | tf_op jit(solution)/shard_map/last_part/pallas_call | solution.py:481
Async XLA Ops:
  1.4 14.6 %collective-permute-start = (bf16[6,104,256]{2,1,0:T(8,128)(2,1)S(1)}, bf16[6,104,256]{2,1,0:T(8,128)(2,1)S(1)}, u32[]{:S(2)}, u32[]{:S(2)}) collective-permute-start(bf16[6,104,256]{2,1,0:T(8,128)(2,1)S(1)} %get-tuple-element.24), channel_id=1, source_target_pairs={{1,33},{3,35},{5,37},{7,39},{9,41},{11,43},{13,45},{15,47},{17,49}... | collective-permute-start | bytes 958472 | tf_op jit(solution)/shard_map/ppermute | solution.py:37
  3.4 12.6 %collective-permute-start.1 = (bf16[6,104,256]{2,1,0:T(8,128)(2,1)S(1)}, bf16[6,104,256]{2,1,0:T(8,128)(2,1)S(1)}, u32[]{:S(2)}, u32[]{:S(2)}) collective-permute-start(bf16[6,104,256]{2,1,0:T(8,128)(2,1)S(1)} %get-tuple-element.25), channel_id=1, source_target_pairs={{0,32},{2,34},{4,36},{6,38},{8,40},{10,42},{12,44},{14,46},{16,48}... | collective-permute-start | bytes 958472 | tf_op jit(solution)/shard_map/ppermute | solution.py:37
  8.5 13.4 %collective-permute-start.2 = (bf16[6,192,128]{2,1,0:T(8,128)(2,1)S(1)}, bf16[6,192,128]{2,1,0:T(8,128)(2,1)S(1)}, u32[]{:S(2)}, u32[]{:S(2)}) collective-permute-start(bf16[6,192,128]{2,1,0:T(8,128)(2,1)S(1)} %get-tuple-element.30), channel_id=1, source_target_pairs={{1,2},{2,1},{3,4},{4,3},{5,6},{6,5},{7,8},{8,7},{9,10},{10,9},{11,... | collective-permute-start | bytes 884744 | tf_op jit(solution)/shard_map/ppermute | solution.py:45
  12.7 9.1 %collective-permute-start.3 = (bf16[6,192,128]{2,1,0:T(8,128)(2,1)S(1)}, bf16[6,192,128]{2,1,0:T(8,128)(2,1)S(1)}, u32[]{:S(2)}, u32[]{:S(2)}) collective-permute-start(bf16[6,192,128]{2,1,0:T(8,128)(2,1)S(1)} %get-tuple-element.31), channel_id=1, source_target_pairs={{0,1},{1,0},{2,3},{3,2},{4,5},{5,4},{6,7},{7,6},{8,9},{9,8},{10,11... | collective-permute-start | bytes 884744 | tf_op jit(solution)/shard_map/ppermute | solution.py:45
  16.3 10.4 %collective-permute-start.4 = (bf16[6,208,128]{2,1,0:T(8,128)(2,1)S(1)}, bf16[6,208,128]{2,1,0:T(8,128)(2,1)S(1)}, u32[]{:S(2)}, u32[]{:S(2)}) collective-permute-start(bf16[6,208,128]{2,1,0:T(8,128)(2,1)S(1)} %get-tuple-element.33), channel_id=1, source_target_pairs={{1,2},{2,1},{3,4},{4,3},{5,6},{6,5},{7,8},{8,7},{9,10},{10,9},{11,... | collective-permute-start | bytes 958472 | tf_op jit(solution)/shard_map/ppermute | solution.py:45
  19.9 6.8 %collective-permute-start.5 = (bf16[6,208,128]{2,1,0:T(8,128)(2,1)S(1)}, bf16[6,208,128]{2,1,0:T(8,128)(2,1)S(1)}, u32[]{:S(2)}, u32[]{:S(2)}) collective-permute-start(bf16[6,208,128]{2,1,0:T(8,128)(2,1)S(1)} %get-tuple-element.34), channel_id=1, source_target_pairs={{0,1},{1,0},{2,3},{3,2},{4,5},{5,4},{6,7},{7,6},{8,9},{9,8},{10,11... | collective-permute-start | bytes 958472 | tf_op jit(solution)/shard_map/ppermute | solution.py:45

commit v4 on v3

--- a/solution.py
+++ b/solution.py
@@ -16,6 +16,7 @@
 SIDE = 128
 CELL_ROWS = 6
 CELL_COLS = 8
+GROUP = KR // (BANDS - 1)
 F32 = jnp.float32
 BF16 = jnp.bfloat16
 VMEM = pl.BlockSpec(memory_space=pltpu.VMEM)
@@ -174,7 +175,17 @@
     )(toa, seed, valid, cloud, land, row_taps, col_taps, tau, adjacency)
 
 
-def toeplitz_kernel(row_ref, col_ref, near_out, far_out, col_out, pad_ref):
+def spread(vector, first):
+    wide = jnp.broadcast_to(vector, (128, 256))
+    return pltpu.roll(wide, first, 1, stride=1, stride_axis=0)
+
+
+def tall(value):
+    swapped = jnp.concatenate([value[0:64, 128:256], value[0:64, 0:128]], axis=1)
+    return jnp.concatenate([value, swapped], axis=0)
+
+
+def toeplitz_kernel(row_ref, col_ref, near_out, taps_out, col_out, pad_ref):
     pad_ref[...] = jnp.zeros_like(pad_ref)
     for band in range(BANDS):
         pad_ref[8 * band : 8 * band + 3, 4 : 4 + TAPS] = row_ref[band]
@@ -185,23 +196,13 @@
     flip = (iota((256, 256), 0) + iota((256, 256), 1) == TAPS + 7).astype(F32).astype(BF16)
     all_flipped = jnp.dot(all_taps, flip, preferred_element_type=F32)
     all_taps = all_taps.astype(F32)
+    taps_out[...] = all_taps
     col_index = iota((384, 128), 1) - iota((384, 128), 0) + (SIDE + KR)
     col_good = (col_index >= 0) & (col_index < TAPS)
     row_at = iota((ROWS, 256), 1)
     row_base = row_at - iota((ROWS, 256), 0)
     near = row_base + KR
     near_good = (near >= 0) & (near < TAPS) & (row_at < ROWS)
-    down_good = row_base + (ROWS + KR) < TAPS
-    above = row_base - (2 * HALO - KR)
-    above_good = (above >= 0) & (above < TAPS) & (row_at < 2 * HALO)
-
-    def spread(vector, first):
-        wide = jnp.broadcast_to(vector, (128, 256))
-        return pltpu.roll(wide, first, 1, stride=1, stride_axis=0)
-
-    def tall(value):
-        swapped = jnp.concatenate([value[0:64, 128:256], value[0:64, 0:128]], axis=1)
-        return jnp.concatenate([value, swapped], axis=0)
 
     for band in range(BANDS):
         for kern in range(3):
@@ -217,11 +218,6 @@
             near_out[band, part, :] = jnp.where(
                 near_good, tall(spread(vector, 152)), 0.0
             ).astype(BF16)
-            far_out[band, part, :] = jnp.where(
-                down_good,
-                tall(spread(vector, 216)),
-                jnp.where(above_good, tall(spread(vector, HALO)), 0.0),
-            ).astype(BF16)
 
 
 def toeplitz(row_taps, col_taps):
@@ -231,7 +227,7 @@
         out_specs=[VMEM] * 3,
         out_shape=vmem_out(
             ((BANDS, 3 * ROWS, 256), BF16),
-            ((BANDS, 3 * ROWS, 256), BF16),
+            ((8 * BANDS, 256), F32),
             ((BANDS, 384, 384), BF16),
         ),
         scratch_shapes=[pltpu.VMEM((8 * BANDS, 256), F32)],
@@ -245,13 +241,23 @@
     del pace
     core = lax.rem(lax.axis_index("across"), 2)
 
-    def fill(up, down, left, right):
-        left[:, 0:HALO] = down[:, :, 0:SIDE]
-        left[:, HALO:] = up[:, :, 0:SIDE]
-        right[:, 0:HALO] = down[:, :, SIDE:]
-        right[:, HALO:] = up[:, :, SIDE:]
+    lane = iota((2 * HALO, SIDE), 1)
+    row = iota((2 * HALO, SIDE), 0)
+    spare = (row >= KR) & (row < 2 * HALO - KR)
+
+    def squeeze(strip, at, keep):
+        part = slice(at, at + SIDE)
+        last = field[BANDS - 1, ROWS:, part].astype(F32)
+        for band in range(BANDS - 1):
+            moved = pltpu.roll(last, KR - GROUP * band, 1)
+            kept = field[band, ROWS:, part].astype(F32)
+            strip[band] = jnp.where(keep, kept, moved).astype(BF16)
+
+    def fill(up, down, to_left, to_right):
         field[:, ROWS : ROWS + HALO] = down[...]
         field[:, ROWS + HALO :] = up[...]
+        squeeze(to_left, 0, (lane < KR) | spare)
+        squeeze(to_right, SIDE, (lane >= SIDE - KR) | spare)
 
     @pl.when(core == 0)
     def _():
@@ -265,12 +271,15 @@
 
 
 def split(toa, early, late, pace):
-    shape = ((BANDS, 2 * HALO, SIDE), BF16)
     return pl.pallas_call(
         split_kernel,
         in_specs=[VMEM] * 4,
         out_specs=[VMEM] * 3,
-        out_shape=vmem_out(shape, shape, ((BANDS, ROWS + 2 * HALO, COLS), BF16)),
+        out_shape=vmem_out(
+            ((BANDS - 1, 2 * HALO, SIDE), BF16),
+            ((BANDS - 1, 2 * HALO, SIDE), BF16),
+            ((BANDS, ROWS + 2 * HALO, COLS), BF16),
+        ),
         compiler_params=pltpu.CompilerParams(vmem_limit_bytes=4 << 20),
         name="split",
     )(toa, early, late, pace)
@@ -293,7 +302,7 @@
     )
 
 
-def own_kernel(field, outer, inner, near_mat, col_mat, env, halo, passed):
+def own_kernel(field, outer, inner, near_mat, col_mat, taps, env, halo, far_out, passed):
     core = lax.rem(lax.axis_index("across"), 2)
     for slot in range(2):
         passed[slot, ROWS:256, :] = jnp.zeros((256 - ROWS, 3 * COLS), BF16)
@@ -314,6 +323,21 @@
             )
             passed[band % 2, 0:ROWS, at] = value.astype(BF16)
 
+    row_at = iota((ROWS, 256), 1)
+    row_base = row_at - iota((ROWS, 256), 0)
+    down_good = row_base + (ROWS + KR) < TAPS
+    above = row_base - (2 * HALO - KR)
+    above_good = (above >= 0) & (above < TAPS) & (row_at < 2 * HALO)
+
+    def far(band):
+        for kern in range(3):
+            vector = taps[8 * band + kern : 8 * band + kern + 1, :]
+            far_out[band, kern * ROWS : (kern + 1) * ROWS, :] = jnp.where(
+                down_good,
+                tall(spread(vector, 216)),
+                jnp.where(above_good, tall(spread(vector, HALO)), 0.0),
+            ).astype(BF16)
+
     def rows(band):
         for kern in range(3):
             at = slice(kern * COLS, (kern + 1) * COLS)
@@ -327,17 +351,20 @@
     for band in range(BANDS):
         if band + 1 < BANDS:
             columns(band + 1)
+        far(band)
         rows(band)
 
 
-def own_part(field, outer, inner, near_mat, col_mat):
+def own_part(field, outer, inner, near_mat, col_mat, taps):
     flops = BANDS * 2 * (192 * 512 * 768 + 208 * 256 * 768 + 192 * 256 * 768)
     return pl.pallas_call(
         own_kernel,
-        in_specs=[VMEM] * 5,
-        out_specs=[VMEM] * 2,
+        in_specs=[VMEM] * 6,
+        out_specs=[VMEM] * 3,
         out_shape=vmem_out(
-            ((BANDS, ROWS, 3 * COLS), F32), ((BANDS, 2 * HALO, 3 * COLS), F32)
+            ((BANDS, ROWS, 3 * COLS), F32),
+            ((BANDS, 2 * HALO, 3 * COLS), F32),
+            ((BANDS, 3 * ROWS, 256), BF16),
         ),
         scratch_shapes=[pltpu.VMEM((2, 256, 3 * COLS), BF16)],
         cost_estimate=pl.CostEstimate(
@@ -345,7 +372,7 @@
         ),
         compiler_params=pltpu.CompilerParams(vmem_limit_bytes=8 << 20),
         name="own_part",
-    )(field, outer, inner, near_mat, col_mat)
+    )(field, outer, inner, near_mat, col_mat, taps)
 
 
 def cell_state(core, cells, field, outer, inner, far_outer, far_inner):
@@ -419,9 +446,22 @@
     for slot in range(2):
         passed[slot, 2 * HALO : 256, :] = jnp.zeros((256 - 2 * HALO, 3 * COLS), BF16)
 
+    lane = iota((2 * HALO, SIDE), 1)
+
+    def last_band(strip, start):
+        value = jnp.zeros((2 * HALO, SIDE), F32)
+        for band in range(BANDS - 1):
+            moved = pltpu.roll(strip[band].astype(F32), SIDE - KR + GROUP * band, 1)
+            value = jnp.where(lane >= start + GROUP * band, moved, value)
+        return value.astype(BF16)
+
     def columns(band):
-        first = far_outer[band]
-        second = far_inner[band]
+        if band + 1 < BANDS:
+            first = far_outer[band]
+            second = far_inner[band]
+        else:
+            first = last_band(far_outer, jnp.where(core == 0, SIDE - KR, 0))
+            second = last_band(far_inner, jnp.where(core == 0, 0, SIDE - KR))
         sides = jnp.concatenate(
             [jnp.where(core == 0, first, second), jnp.where(core == 0, second, first)], axis=1
         )
@@ -507,11 +547,11 @@
     late = exchange(to_late, -1)
     outer = swap(to_outer, 1)
     inner = swap(to_inner, 0)
-    near_mat, far_mat, col_mat = toeplitz(row_taps, col_taps)
+    near_mat, taps, col_mat = toeplitz(row_taps, col_taps)
     far_to_outer, far_to_inner, field = split(toa, early, late, near_mat)
     far_outer = swap(far_to_outer, 1)
     far_inner = swap(far_to_inner, 0)
-    env, halo = own_part(field, outer, inner, near_mat, col_mat)
+    env, halo, far_mat = own_part(field, outer, inner, near_mat, col_mat, taps)
     return last_part(
         scales, field, outer, inner, cells, far_outer, far_inner,
         far_mat, col_mat, env, halo,

time: 29.3 us -> 28.6 us (0.976)
  waiting for transfers between devices: 2.65 us -> 1.78 us
  starting transfers between devices: 18.8 us -> 19.1 us
    ppermute x4, waiting for transfers between devices: 2.64 us -> 1.78 us  [swap(): return lax.ppermute(value, 'across', pairs)]
where the time goes in v4:
time: 28.6 us; the launch traced here: 28.2 us
  starting transfers between devices  19.1 us (67%)
  Pallas kernels  7.28 us (25%)
  waiting for transfers between devices  1.78 us (6%)
    ppermute x4, starting transfers between devices, swap(): return lax.ppermute(value, 'across', pairs)  12 us
    ppermute x2, starting transfers between devices, exchange(): return lax.ppermute(value, ('along', 'across'), pairs)  7.05 us
    pallas_call x1, Pallas kernels, last_part(): pl.pallas_call(last_kernel, in_specs=[VMEM] * 11, out_specs=pl.BlockSpec(...  2.3 us
    pallas_call x1, Pallas kernels, own_part(): pl.pallas_call(own_kernel, in_specs=[VMEM] * 6, out_specs=[VMEM] * 3, out...  2.19 us
    ppermute x4, waiting for transfers between devices, swap(): return lax.ppermute(value, 'across', pairs)  1.78 us
    pallas_call x1, Pallas kernels, pack(): pl.pallas_call(pack_kernel, in_specs=[pl.BlockSpec(memory_space=pltpu.HBM...  1.4 us
    pallas_call x1, Pallas kernels, toeplitz(): pl.pallas_call(toeplitz_kernel, in_specs=[VMEM] * 2, out_specs=[VMEM] * 3...  1.11 us
  transfers between devices with their start and end apart: 6, of which 1 were waited for; matrix products, arithmetic and copies ran while one was open for 0% of the time, Pallas kernels for 13%

profile of v4, /device:TPU:102, one launch (start us, length us, event | category | flops | bytes accessed | tf_op | source)
XLA Modules:
  0.0 28.2 jit_solution(11240674396178050515)
XLA Ops:
  0.0 1.4 %pack.1 = (bf16[6,104,256]{2,1,0:T(8,128)(2,1)S(1)}, bf16[6,104,256]{2,1,0:T(8,128)(2,1)S(1)}, bf16[6,192,128]{2,1,0:T(8,128)(2,1)S(1)}, bf16[6,192,128]{2,1,0:T...) custom-call(bf16[6,192,256]{2,1,0:T(8,128)(2,1)} %toa_in.1, ...), custom_call_target="tpu_custom_call" | custom-call | tf_op jit(solution)/shard_map/pack/pallas_call | solution.py:148
  1.4 2.0 %collective-permute-start = (bf16[6,104,256]{2,1,0:T(8,128)(2,1)S(1)}, bf16[6,104,256]{2,1,0:T(8,128)(2,1)S(1)}, u32[]{:S(2)}, u32[]{:S(2)}) collective-permute-start(bf16[6,104,256]{2,1,0:T(8,128)(2,1)S(1)} %get-tuple-element.25), channel_id=1, source_target_pairs={{1,33},{3,35},{5,37},{7,39},{9,41},{11,43},{13,45},{15,47},{17,49}... | collective-permute-start | bytes 958472 | tf_op jit(solution)/shard_map/ppermute | solution.py:38
  3.4 5.0 %collective-permute-start.1 = (bf16[6,104,256]{2,1,0:T(8,128)(2,1)S(1)}, bf16[6,104,256]{2,1,0:T(8,128)(2,1)S(1)}, u32[]{:S(2)}, u32[]{:S(2)}) collective-permute-start(bf16[6,104,256]{2,1,0:T(8,128)(2,1)S(1)} %get-tuple-element.26), channel_id=1, source_target_pairs={{0,32},{2,34},{4,36},{6,38},{8,40},{10,42},{12,44},{14,46},{16,48}... | collective-permute-start | bytes 958472 | tf_op jit(solution)/shard_map/ppermute | solution.py:38
  8.5 4.2 %collective-permute-start.2 = (bf16[6,192,128]{2,1,0:T(8,128)(2,1)S(1)}, bf16[6,192,128]{2,1,0:T(8,128)(2,1)S(1)}, u32[]{:S(2)}, u32[]{:S(2)}) collective-permute-start(bf16[6,192,128]{2,1,0:T(8,128)(2,1)S(1)} %get-tuple-element.31), channel_id=1, source_target_pairs={{1,2},{2,1},{3,4},{4,3},{5,6},{6,5},{7,8},{8,7},{9,10},{10,9},{11,... | collective-permute-start | bytes 884744 | tf_op jit(solution)/shard_map/ppermute | solution.py:46
  12.7 1.9 %collective-permute-start.3 = (bf16[6,192,128]{2,1,0:T(8,128)(2,1)S(1)}, bf16[6,192,128]{2,1,0:T(8,128)(2,1)S(1)}, u32[]{:S(2)}, u32[]{:S(2)}) collective-permute-start(bf16[6,192,128]{2,1,0:T(8,128)(2,1)S(1)} %get-tuple-element.32), channel_id=1, source_target_pairs={{0,1},{1,0},{2,3},{3,2},{4,5},{5,4},{6,7},{7,6},{8,9},{9,8},{10,11... | collective-permute-start | bytes 884744 | tf_op jit(solution)/shard_map/ppermute | solution.py:46
  14.7 1.1 %toeplitz.1 = (bf16[6,576,256]{2,1,0:T(8,128)(2,1)S(1)}, f32[48,256]{1,0:T(8,128)S(1)}, bf16[6,384,384]{2,1,0:T(8,128)(2,1)S(1)}) custom-call(f32[6,3,201]{2,1,0:T(4,128)S(1)} %get-tuple-element.27.row_ref, f32[6,3,201]{2,1,0:T(4,128)S(1)} %get-tuple-element.28.col_ref), custom_call_target="tpu_custom_call" | custom-call | bytes 8000000 | tf_op jit(solution)/shard_map/toeplitz/pallas_call | solution.py:224
  15.8 0.0 collective-permute-done.early
  15.8 0.0 collective-permute-done.1.late
  15.8 0.3 split.1
  16.1 3.9 %collective-permute-start.4 = (bf16[5,208,128]{2,1,0:T(8,128)(2,1)S(1)}, bf16[5,208,128]{2,1,0:T(8,128)(2,1)S(1)}, u32[]{:S(2)}, u32[]{:S(2)}) collective-permute-start(bf16[5,208,128]{2,1,0:T(8,128)(2,1)S(1)} %get-tuple-element.34), channel_id=1, source_target_pairs={{1,2},{2,1},{3,4},{4,3},{5,6},{6,5},{7,8},{8,7},{9,10},{10,9},{11,... | collective-permute-start | bytes 798728 | tf_op jit(solution)/shard_map/ppermute | solution.py:46
  20.0 1.9 %collective-permute-start.5 = (bf16[5,208,128]{2,1,0:T(8,128)(2,1)S(1)}, bf16[5,208,128]{2,1,0:T(8,128)(2,1)S(1)}, u32[]{:S(2)}, u32[]{:S(2)}) collective-permute-start(bf16[5,208,128]{2,1,0:T(8,128)(2,1)S(1)} %get-tuple-element.35), channel_id=1, source_target_pairs={{0,1},{1,0},{2,3},{3,2},{4,5},{5,4},{6,7},{7,6},{8,9},{9,8},{10,11... | collective-permute-start | bytes 798728 | tf_op jit(solution)/shard_map/ppermute | solution.py:46
  21.9 0.0 collective-permute-done.2.outer
  22.0 0.0 collective-permute-done.3.inner
  22.0 2.2 %own_part.1 = (f32[6,192,768]{2,1,0:T(8,128)S(1)}, f32[6,208,768]{2,1,0:T(8,128)S(1)}, bf16[6,576,256]{2,1,0:T(8,128)(2,1)S(1)}) custom-call(bf16[6,400,256]{2,1,0:T(8,128)(2,1)S(1)} %get-tuple-element.30.field, bf16[6,192,128]{2,1,0:T(8,128)(2,1)S(1)} %collective-permute-done.2.outer, bf16[6,192,128]{2,1,0:T(8,128)(2,1)S(1)} %collective-permute-done.3.inner, ...), custom_call_target="tpu_custom_call" | custom-call | flops 1849688064 | bytes 10000000 | tf_op jit(solution)/shard_map/own_part/pallas_call | solution.py:360
  24.2 1.8 %collective-permute-done.4.far_outer = bf16[5,208,128]{2,1,0:T(8,128)(2,1)S(1)} collective-permute-done((bf16[5,208,128]{2,1,0:T(8,128)(2,1)S(1)}, bf16[5,208,128]{2,1,0:T(8,128)(2,1)S(1)}, u32[]{:S(2)}, u32[]{:S(2)}) %collective-permute-start.4) | collective-permute-done | bytes 266272 | tf_op jit(solution)/shard_map/ppermute | solution.py:46
  25.9 0.0 collective-permute-done.5.far_inner
  25.9 2.3 %last_part.1 = f32[6,192,256]{2,1,0:T(8,128)} custom-call(f32[16,256]{1,0:T(8,128)S(1)} %get-tuple-element.23.scales, bf16[6,400,256]{2,1,0:T(8,128)(2,1)S(1)} %get-tuple-element.30.field, bf16[6,192,128]{2,1,0:T(8,128)(2,1)S(1)} %collective-permute-done.2.outer, bf16[6,192,128]{2,1,0:T(8,128)(2,1)S(1)} %collective-permute-done.3.inner, ...), custom_call_target="tpu_custom_call" | custom-call | flops 943718400 | bytes 12000000 | tf_op jit(solution)/shard_map/last_part/pallas_call | solution.py:521
Async XLA Ops:
  1.4 14.4 %collective-permute-start = (bf16[6,104,256]{2,1,0:T(8,128)(2,1)S(1)}, bf16[6,104,256]{2,1,0:T(8,128)(2,1)S(1)}, u32[]{:S(2)}, u32[]{:S(2)}) collective-permute-start(bf16[6,104,256]{2,1,0:T(8,128)(2,1)S(1)} %get-tuple-element.25), channel_id=1, source_target_pairs={{1,33},{3,35},{5,37},{7,39},{9,41},{11,43},{13,45},{15,47},{17,49}... | collective-permute-start | bytes 958472 | tf_op jit(solution)/shard_map/ppermute | solution.py:38
  3.4 12.4 %collective-permute-start.1 = (bf16[6,104,256]{2,1,0:T(8,128)(2,1)S(1)}, bf16[6,104,256]{2,1,0:T(8,128)(2,1)S(1)}, u32[]{:S(2)}, u32[]{:S(2)}) collective-permute-start(bf16[6,104,256]{2,1,0:T(8,128)(2,1)S(1)} %get-tuple-element.26), channel_id=1, source_target_pairs={{0,32},{2,34},{4,36},{6,38},{8,40},{10,42},{12,44},{14,46},{16,48}... | collective-permute-start | bytes 958472 | tf_op jit(solution)/shard_map/ppermute | solution.py:38
  8.5 13.5 %collective-permute-start.2 = (bf16[6,192,128]{2,1,0:T(8,128)(2,1)S(1)}, bf16[6,192,128]{2,1,0:T(8,128)(2,1)S(1)}, u32[]{:S(2)}, u32[]{:S(2)}) collective-permute-start(bf16[6,192,128]{2,1,0:T(8,128)(2,1)S(1)} %get-tuple-element.31), channel_id=1, source_target_pairs={{1,2},{2,1},{3,4},{4,3},{5,6},{6,5},{7,8},{8,7},{9,10},{10,9},{11,... | collective-permute-start | bytes 884744 | tf_op jit(solution)/shard_map/ppermute | solution.py:46
  12.7 9.2 %collective-permute-start.3 = (bf16[6,192,128]{2,1,0:T(8,128)(2,1)S(1)}, bf16[6,192,128]{2,1,0:T(8,128)(2,1)S(1)}, u32[]{:S(2)}, u32[]{:S(2)}) collective-permute-start(bf16[6,192,128]{2,1,0:T(8,128)(2,1)S(1)} %get-tuple-element.32), channel_id=1, source_target_pairs={{0,1},{1,0},{2,3},{3,2},{4,5},{5,4},{6,7},{7,6},{8,9},{9,8},{10,11... | collective-permute-start | bytes 884744 | tf_op jit(solution)/shard_map/ppermute | solution.py:46
  16.1 9.8 %collective-permute-start.4 = (bf16[5,208,128]{2,1,0:T(8,128)(2,1)S(1)}, bf16[5,208,128]{2,1,0:T(8,128)(2,1)S(1)}, u32[]{:S(2)}, u32[]{:S(2)}) collective-permute-start(bf16[5,208,128]{2,1,0:T(8,128)(2,1)S(1)} %get-tuple-element.34), channel_id=1, source_target_pairs={{1,2},{2,1},{3,4},{4,3},{5,6},{6,5},{7,8},{8,7},{9,10},{10,9},{11,... | collective-permute-start | bytes 798728 | tf_op jit(solution)/shard_map/ppermute | solution.py:46
  20.0 5.9 %collective-permute-start.5 = (bf16[5,208,128]{2,1,0:T(8,128)(2,1)S(1)}, bf16[5,208,128]{2,1,0:T(8,128)(2,1)S(1)}, u32[]{:S(2)}, u32[]{:S(2)}) collective-permute-start(bf16[5,208,128]{2,1,0:T(8,128)(2,1)S(1)} %get-tuple-element.35), channel_id=1, source_target_pairs={{0,1},{1,0},{2,3},{3,2},{4,5},{5,4},{6,7},{7,6},{8,9},{9,8},{10,11... | collective-permute-start | bytes 798728 | tf_op jit(solution)/shard_map/ppermute | solution.py:46

commit v5 on v4

--- a/solution.py
+++ b/solution.py
@@ -237,8 +237,7 @@
     )(row_taps, col_taps)
 
 
-def split_kernel(toa, early, late, pace, outer, inner, field):
-    del pace
+def split_kernel(toa, early, late, outer, inner, field):
     core = lax.rem(lax.axis_index("across"), 2)
 
     lane = iota((2 * HALO, SIDE), 1)
@@ -270,10 +269,10 @@
     field[:, 0:ROWS] = toa[...]
 
 
-def split(toa, early, late, pace):
+def split(toa, early, late):
     return pl.pallas_call(
         split_kernel,
-        in_specs=[VMEM] * 4,
+        in_specs=[VMEM] * 3,
         out_specs=[VMEM] * 3,
         out_shape=vmem_out(
             ((BANDS - 1, 2 * HALO, SIDE), BF16),
@@ -282,7 +281,7 @@
         ),
         compiler_params=pltpu.CompilerParams(vmem_limit_bytes=4 << 20),
         name="split",
-    )(toa, early, late, pace)
+    )(toa, early, late)
 
 
 def middle_matrix(col_mat, band, kern):
@@ -548,7 +547,7 @@
     outer = swap(to_outer, 1)
     inner = swap(to_inner, 0)
     near_mat, taps, col_mat = toeplitz(row_taps, col_taps)
-    far_to_outer, far_to_inner, field = split(toa, early, late, near_mat)
+    far_to_outer, far_to_inner, field = split(toa, early, late)
     far_outer = swap(far_to_outer, 1)
     far_inner = swap(far_to_inner, 0)
     env, halo, far_mat = own_part(field, outer, inner, near_mat, col_mat, taps)

time: 28.6 us -> 28.6 us (level)
  the two profiles are of different devices: /device:TPU:102 before, /device:TPU:103 now
where the time goes in v5:
time: 28.6 us; the launch traced here: 28.3 us
  starting transfers between devices  20.9 us (73%)
  Pallas kernels  7.29 us (25%)
    ppermute x4, starting transfers between devices, swap(): return lax.ppermute(value, 'across', pairs)  14.2 us
    ppermute x2, starting transfers between devices, exchange(): return lax.ppermute(value, ('along', 'across'), pairs)  6.68 us
    pallas_call x1, Pallas kernels, last_part(): pl.pallas_call(last_kernel, in_specs=[VMEM] * 11, out_specs=pl.BlockSpec(...  2.29 us
    pallas_call x1, Pallas kernels, own_part(): pl.pallas_call(own_kernel, in_specs=[VMEM] * 6, out_specs=[VMEM] * 3, out...  2.22 us
    pallas_call x1, Pallas kernels, pack(): pl.pallas_call(pack_kernel, in_specs=[pl.BlockSpec(memory_space=pltpu.HBM...  1.39 us
    pallas_call x1, Pallas kernels, toeplitz(): pl.pallas_call(toeplitz_kernel, in_specs=[VMEM] * 2, out_specs=[VMEM] * 3...  1.11 us
  transfers between devices with their start and end apart: 6, of which 0 were waited for; matrix products, arithmetic and copies ran while one was open for 0% of the time, Pallas kernels for 13%

profile of v5, /device:TPU:103, one launch (start us, length us, event | category | flops | bytes accessed | tf_op | source)
XLA Modules:
  0.0 28.3 jit_solution(10166621733130931779)
XLA Ops:
  0.0 1.4 %pack.1 = (bf16[6,104,256]{2,1,0:T(8,128)(2,1)S(1)}, bf16[6,104,256]{2,1,0:T(8,128)(2,1)S(1)}, bf16[6,192,128]{2,1,0:T(8,128)(2,1)S(1)}, bf16[6,192,128]{2,1,0:T...) custom-call(bf16[6,192,256]{2,1,0:T(8,128)(2,1)} %toa_in.1, ...), custom_call_target="tpu_custom_call" | custom-call | tf_op jit(solution)/shard_map/pack/pallas_call | solution.py:148
  1.4 4.8 %collective-permute-start = (bf16[6,104,256]{2,1,0:T(8,128)(2,1)S(1)}, bf16[6,104,256]{2,1,0:T(8,128)(2,1)S(1)}, u32[]{:S(2)}, u32[]{:S(2)}) collective-permute-start(bf16[6,104,256]{2,1,0:T(8,128)(2,1)S(1)} %get-tuple-element.25), channel_id=1, source_target_pairs={{1,33},{3,35},{5,37},{7,39},{9,41},{11,43},{13,45},{15,47},{17,49}... | collective-permute-start | bytes 958472 | tf_op jit(solution)/shard_map/ppermute | solution.py:38
  6.2 1.9 %collective-permute-start.1 = (bf16[6,104,256]{2,1,0:T(8,128)(2,1)S(1)}, bf16[6,104,256]{2,1,0:T(8,128)(2,1)S(1)}, u32[]{:S(2)}, u32[]{:S(2)}) collective-permute-start(bf16[6,104,256]{2,1,0:T(8,128)(2,1)S(1)} %get-tuple-element.26), channel_id=1, source_target_pairs={{0,32},{2,34},{4,36},{6,38},{8,40},{10,42},{12,44},{14,46},{16,48}... | collective-permute-start | bytes 958472 | tf_op jit(solution)/shard_map/ppermute | solution.py:38
  8.1 4.1 %collective-permute-start.2 = (bf16[6,192,128]{2,1,0:T(8,128)(2,1)S(1)}, bf16[6,192,128]{2,1,0:T(8,128)(2,1)S(1)}, u32[]{:S(2)}, u32[]{:S(2)}) collective-permute-start(bf16[6,192,128]{2,1,0:T(8,128)(2,1)S(1)} %get-tuple-element.28), channel_id=1, source_target_pairs={{1,2},{2,1},{3,4},{4,3},{5,6},{6,5},{7,8},{8,7},{9,10},{10,9},{11,... | collective-permute-start | bytes 884744 | tf_op jit(solution)/shard_map/ppermute | solution.py:46
  12.2 3.1 %collective-permute-start.3 = (bf16[6,192,128]{2,1,0:T(8,128)(2,1)S(1)}, bf16[6,192,128]{2,1,0:T(8,128)(2,1)S(1)}, u32[]{:S(2)}, u32[]{:S(2)}) collective-permute-start(bf16[6,192,128]{2,1,0:T(8,128)(2,1)S(1)} %get-tuple-element.29), channel_id=1, source_target_pairs={{0,1},{1,0},{2,3},{3,2},{4,5},{5,4},{6,7},{7,6},{8,9},{9,8},{10,11... | collective-permute-start | bytes 884744 | tf_op jit(solution)/shard_map/ppermute | solution.py:46
  15.3 0.0 collective-permute-done.early
  15.3 0.0 collective-permute-done.1.late
  15.3 0.3 split.1
  15.6 2.4 %collective-permute-start.4 = (bf16[5,208,128]{2,1,0:T(8,128)(2,1)S(1)}, bf16[5,208,128]{2,1,0:T(8,128)(2,1)S(1)}, u32[]{:S(2)}, u32[]{:S(2)}) collective-permute-start(bf16[5,208,128]{2,1,0:T(8,128)(2,1)S(1)} %get-tuple-element.31), channel_id=1, source_target_pairs={{1,2},{2,1},{3,4},{4,3},{5,6},{6,5},{7,8},{8,7},{9,10},{10,9},{11,... | collective-permute-start | bytes 798728 | tf_op jit(solution)/shard_map/ppermute | solution.py:46
  18.1 4.5 %collective-permute-start.5 = (bf16[5,208,128]{2,1,0:T(8,128)(2,1)S(1)}, bf16[5,208,128]{2,1,0:T(8,128)(2,1)S(1)}, u32[]{:S(2)}, u32[]{:S(2)}) collective-permute-start(bf16[5,208,128]{2,1,0:T(8,128)(2,1)S(1)} %get-tuple-element.32), channel_id=1, source_target_pairs={{0,1},{1,0},{2,3},{3,2},{4,5},{5,4},{6,7},{7,6},{8,9},{9,8},{10,11... | collective-permute-start | bytes 798728 | tf_op jit(solution)/shard_map/ppermute | solution.py:46
  22.6 1.1 %toeplitz.1 = (bf16[6,576,256]{2,1,0:T(8,128)(2,1)S(1)}, f32[48,256]{1,0:T(8,128)S(1)}, bf16[6,384,384]{2,1,0:T(8,128)(2,1)S(1)}) custom-call(f32[6,3,201]{2,1,0:T(4,128)S(1)} %get-tuple-element.33.row_ref, f32[6,3,201]{2,1,0:T(4,128)S(1)} %get-tuple-element.34.col_ref), custom_call_target="tpu_custom_call" | custom-call | bytes 8000000 | tf_op jit(solution)/shard_map/toeplitz/pallas_call | solution.py:224
  23.7 0.0 collective-permute-done.2.outer
  23.7 0.0 collective-permute-done.3.inner
  23.7 2.2 %own_part.1 = (f32[6,192,768]{2,1,0:T(8,128)S(1)}, f32[6,208,768]{2,1,0:T(8,128)S(1)}, bf16[6,576,256]{2,1,0:T(8,128)(2,1)S(1)}) custom-call(bf16[6,400,256]{2,1,0:T(8,128)(2,1)S(1)} %get-tuple-element.27.field, bf16[6,192,128]{2,1,0:T(8,128)(2,1)S(1)} %collective-permute-done.2.outer, bf16[6,192,128]{2,1,0:T(8,128)(2,1)S(1)} %collective-permute-done.3.inner, ...), custom_call_target="tpu_custom_call" | custom-call | flops 1849688064 | bytes 10000000 | tf_op jit(solution)/shard_map/own_part/pallas_call | solution.py:359
  26.0 0.0 collective-permute-done.4.far_outer
  26.0 0.0 collective-permute-done.5.far_inner
  26.0 2.3 %last_part.1 = f32[6,192,256]{2,1,0:T(8,128)} custom-call(f32[16,256]{1,0:T(8,128)S(1)} %get-tuple-element.23.scales, bf16[6,400,256]{2,1,0:T(8,128)(2,1)S(1)} %get-tuple-element.27.field, bf16[6,192,128]{2,1,0:T(8,128)(2,1)S(1)} %collective-permute-done.2.outer, bf16[6,192,128]{2,1,0:T(8,128)(2,1)S(1)} %collective-permute-done.3.inner, ...), custom_call_target="tpu_custom_call" | custom-call | flops 943718400 | bytes 12000000 | tf_op jit(solution)/shard_map/last_part/pallas_call | solution.py:520
Async XLA Ops:
  1.4 13.9 %collective-permute-start = (bf16[6,104,256]{2,1,0:T(8,128)(2,1)S(1)}, bf16[6,104,256]{2,1,0:T(8,128)(2,1)S(1)}, u32[]{:S(2)}, u32[]{:S(2)}) collective-permute-start(bf16[6,104,256]{2,1,0:T(8,128)(2,1)S(1)} %get-tuple-element.25), channel_id=1, source_target_pairs={{1,33},{3,35},{5,37},{7,39},{9,41},{11,43},{13,45},{15,47},{17,49}... | collective-permute-start | bytes 958472 | tf_op jit(solution)/shard_map/ppermute | solution.py:38
  6.2 9.2 %collective-permute-start.1 = (bf16[6,104,256]{2,1,0:T(8,128)(2,1)S(1)}, bf16[6,104,256]{2,1,0:T(8,128)(2,1)S(1)}, u32[]{:S(2)}, u32[]{:S(2)}) collective-permute-start(bf16[6,104,256]{2,1,0:T(8,128)(2,1)S(1)} %get-tuple-element.26), channel_id=1, source_target_pairs={{0,32},{2,34},{4,36},{6,38},{8,40},{10,42},{12,44},{14,46},{16,48}... | collective-permute-start | bytes 958472 | tf_op jit(solution)/shard_map/ppermute | solution.py:38
  8.1 15.6 %collective-permute-start.2 = (bf16[6,192,128]{2,1,0:T(8,128)(2,1)S(1)}, bf16[6,192,128]{2,1,0:T(8,128)(2,1)S(1)}, u32[]{:S(2)}, u32[]{:S(2)}) collective-permute-start(bf16[6,192,128]{2,1,0:T(8,128)(2,1)S(1)} %get-tuple-element.28), channel_id=1, source_target_pairs={{1,2},{2,1},{3,4},{4,3},{5,6},{6,5},{7,8},{8,7},{9,10},{10,9},{11,... | collective-permute-start | bytes 884744 | tf_op jit(solution)/shard_map/ppermute | solution.py:46
  12.2 11.5 %collective-permute-start.3 = (bf16[6,192,128]{2,1,0:T(8,128)(2,1)S(1)}, bf16[6,192,128]{2,1,0:T(8,128)(2,1)S(1)}, u32[]{:S(2)}, u32[]{:S(2)}) collective-permute-start(bf16[6,192,128]{2,1,0:T(8,128)(2,1)S(1)} %get-tuple-element.29), channel_id=1, source_target_pairs={{0,1},{1,0},{2,3},{3,2},{4,5},{5,4},{6,7},{7,6},{8,9},{9,8},{10,11... | collective-permute-start | bytes 884744 | tf_op jit(solution)/shard_map/ppermute | solution.py:46
  15.6 10.3 %collective-permute-start.4 = (bf16[5,208,128]{2,1,0:T(8,128)(2,1)S(1)}, bf16[5,208,128]{2,1,0:T(8,128)(2,1)S(1)}, u32[]{:S(2)}, u32[]{:S(2)}) collective-permute-start(bf16[5,208,128]{2,1,0:T(8,128)(2,1)S(1)} %get-tuple-element.31), channel_id=1, source_target_pairs={{1,2},{2,1},{3,4},{4,3},{5,6},{6,5},{7,8},{8,7},{9,10},{10,9},{11,... | collective-permute-start | bytes 798728 | tf_op jit(solution)/shard_map/ppermute | solution.py:46
  18.1 7.9 %collective-permute-start.5 = (bf16[5,208,128]{2,1,0:T(8,128)(2,1)S(1)}, bf16[5,208,128]{2,1,0:T(8,128)(2,1)S(1)}, u32[]{:S(2)}, u32[]{:S(2)}) collective-permute-start(bf16[5,208,128]{2,1,0:T(8,128)(2,1)S(1)} %get-tuple-element.32), channel_id=1, source_target_pairs={{0,1},{1,0},{2,3},{3,2},{4,5},{5,4},{6,7},{7,6},{8,9},{9,8},{10,11... | collective-permute-start | bytes 798728 | tf_op jit(solution)/shard_map/ppermute | solution.py:46

commit v6 on v5

--- a/solution.py
+++ b/solution.py
@@ -303,7 +303,7 @@
 
 def own_kernel(field, outer, inner, near_mat, col_mat, taps, env, halo, far_out, passed):
     core = lax.rem(lax.axis_index("across"), 2)
-    for slot in range(2):
+    for slot in range(3):
         passed[slot, ROWS:256, :] = jnp.zeros((256 - ROWS, 3 * COLS), BF16)
 
     def columns(band):
@@ -320,7 +320,7 @@
             value = value[0:ROWS] + jnp.dot(
                 sides, side_matrix(col_mat, band, kern), preferred_element_type=F32
             )
-            passed[band % 2, 0:ROWS, at] = value.astype(BF16)
+            passed[band % 3, 0:ROWS, at] = value.astype(BF16)
 
     row_at = iota((ROWS, 256), 1)
     row_base = row_at - iota((ROWS, 256), 0)
@@ -342,14 +342,15 @@
             at = slice(kern * COLS, (kern + 1) * COLS)
             env[band, :, at] = jnp.dot(
                 near_mat[band, kern * ROWS : (kern + 1) * ROWS, :],
-                passed[band % 2, :, at],
+                passed[band % 3, :, at],
                 preferred_element_type=F32,
             )
 
     columns(0)
+    columns(1)
     for band in range(BANDS):
-        if band + 1 < BANDS:
-            columns(band + 1)
+        if band + 2 < BANDS:
+            columns(band + 2)
         far(band)
         rows(band)
 
@@ -365,7 +366,7 @@
             ((BANDS, 2 * HALO, 3 * COLS), F32),
             ((BANDS, 3 * ROWS, 256), BF16),
         ),
-        scratch_shapes=[pltpu.VMEM((2, 256, 3 * COLS), BF16)],
+        scratch_shapes=[pltpu.VMEM((3, 256, 3 * COLS), BF16)],
         cost_estimate=pl.CostEstimate(
             flops=flops, bytes_accessed=10_000_000, transcendentals=0
         ),
@@ -442,7 +443,7 @@
     far_mat, col_mat, env, halo, out, passed, result, sems,
 ):
     core = lax.rem(lax.axis_index("across"), 2)
-    for slot in range(2):
+    for slot in range(3):
         passed[slot, 2 * HALO : 256, :] = jnp.zeros((256 - 2 * HALO, 3 * COLS), BF16)
 
     lane = iota((2 * HALO, SIDE), 1)
@@ -469,9 +470,10 @@
             value = jnp.dot(
                 sides, side_matrix(col_mat, band, kern), preferred_element_type=F32
             )
-            passed[band % 2, 0 : 2 * HALO, at] = (value + halo[band, :, at]).astype(BF16)
+            passed[band % 3, 0 : 2 * HALO, at] = (value + halo[band, :, at]).astype(BF16)
 
     columns(0)
+    columns(1)
     small = cell_state(core, cells, field, outer, inner, far_outer, far_inner)
     block = iota((8, COLS), 1) // CB
     aot = jnp.zeros((8, COLS), F32)
@@ -488,8 +490,8 @@
         return pltpu.make_async_copy(result.at[band], out.at[band], sems.at[band])
 
     for band in range(BANDS):
-        if band + 1 < BANDS:
-            columns(band + 1)
+        if band + 2 < BANDS:
+            columns(band + 2)
         growth = jnp.exp(scales[band : band + 1, :] * aot)
         strength = scales[8 + band : 9 + band, :]
         own = (1.0 + strength) * growth
@@ -499,7 +501,7 @@
             env[band, :, kern * COLS : (kern + 1) * COLS]
             + jnp.dot(
                 far_mat[band, kern * ROWS : (kern + 1) * ROWS, :],
-                passed[band % 2, :, kern * COLS : (kern + 1) * COLS],
+                passed[band % 3, :, kern * COLS : (kern + 1) * COLS],
                 preferred_element_type=F32,
             )
             for kern in range(3)
@@ -523,7 +525,7 @@
         out_specs=pl.BlockSpec(memory_space=pl.ANY),
         out_shape=jax.ShapeDtypeStruct((BANDS, ROWS, COLS), F32),
         scratch_shapes=[
-            pltpu.VMEM((2, 256, 3 * COLS), BF16),
+            pltpu.VMEM((3, 256, 3 * COLS), BF16),
             pltpu.VMEM((BANDS, ROWS, COLS), F32),
             pltpu.SemaphoreType.DMA((BANDS,)),
         ],

time: 28.6 us -> 28.5 us (level)
  no operation moved by 1% of the time
where the time goes in v6:
time: 28.5 us; the launch traced here: 28.2 us
  starting transfers between devices  20.9 us (73%)
  Pallas kernels  7.23 us (25%)
    ppermute x4, starting transfers between devices, swap(): return lax.ppermute(value, 'across', pairs)  14.2 us
    ppermute x2, starting transfers between devices, exchange(): return lax.ppermute(value, ('along', 'across'), pairs)  6.68 us
    pallas_call x1, Pallas kernels, last_part(): pl.pallas_call(last_kernel, in_specs=[VMEM] * 11, out_specs=pl.BlockSpec(...  2.27 us
    pallas_call x1, Pallas kernels, own_part(): pl.pallas_call(own_kernel, in_specs=[VMEM] * 6, out_specs=[VMEM] * 3, out...  2.17 us
    pallas_call x1, Pallas kernels, pack(): pl.pallas_call(pack_kernel, in_specs=[pl.BlockSpec(memory_space=pltpu.HBM...  1.39 us
    pallas_call x1, Pallas kernels, toeplitz(): pl.pallas_call(toeplitz_kernel, in_specs=[VMEM] * 2, out_specs=[VMEM] * 3...  1.11 us
  transfers between devices with their start and end apart: 6, of which 0 were waited for; matrix products, arithmetic and copies ran while one was open for 0% of the time, Pallas kernels for 13%

profile of v6, /device:TPU:103, one launch (start us, length us, event | category | flops | bytes accessed | tf_op | source)
XLA Modules:
  0.0 28.2 jit_solution(10727974335165883354)
XLA Ops:
  0.0 1.4 %pack.1 = (bf16[6,104,256]{2,1,0:T(8,128)(2,1)S(1)}, bf16[6,104,256]{2,1,0:T(8,128)(2,1)S(1)}, bf16[6,192,128]{2,1,0:T(8,128)(2,1)S(1)}, bf16[6,192,128]{2,1,0:T...) custom-call(bf16[6,192,256]{2,1,0:T(8,128)(2,1)} %toa_in.1, ...), custom_call_target="tpu_custom_call" | custom-call | tf_op jit(solution)/shard_map/pack/pallas_call | solution.py:148
  1.4 4.8 %collective-permute-start = (bf16[6,104,256]{2,1,0:T(8,128)(2,1)S(1)}, bf16[6,104,256]{2,1,0:T(8,128)(2,1)S(1)}, u32[]{:S(2)}, u32[]{:S(2)}) collective-permute-start(bf16[6,104,256]{2,1,0:T(8,128)(2,1)S(1)} %get-tuple-element.25), channel_id=1, source_target_pairs={{1,33},{3,35},{5,37},{7,39},{9,41},{11,43},{13,45},{15,47},{17,49}... | collective-permute-start | bytes 958472 | tf_op jit(solution)/shard_map/ppermute | solution.py:38
  6.2 1.9 %collective-permute-start.1 = (bf16[6,104,256]{2,1,0:T(8,128)(2,1)S(1)}, bf16[6,104,256]{2,1,0:T(8,128)(2,1)S(1)}, u32[]{:S(2)}, u32[]{:S(2)}) collective-permute-start(bf16[6,104,256]{2,1,0:T(8,128)(2,1)S(1)} %get-tuple-element.26), channel_id=1, source_target_pairs={{0,32},{2,34},{4,36},{6,38},{8,40},{10,42},{12,44},{14,46},{16,48}... | collective-permute-start | bytes 958472 | tf_op jit(solution)/shard_map/ppermute | solution.py:38
  8.1 4.1 %collective-permute-start.2 = (bf16[6,192,128]{2,1,0:T(8,128)(2,1)S(1)}, bf16[6,192,128]{2,1,0:T(8,128)(2,1)S(1)}, u32[]{:S(2)}, u32[]{:S(2)}) collective-permute-start(bf16[6,192,128]{2,1,0:T(8,128)(2,1)S(1)} %get-tuple-element.28), channel_id=1, source_target_pairs={{1,2},{2,1},{3,4},{4,3},{5,6},{6,5},{7,8},{8,7},{9,10},{10,9},{11,... | collective-permute-start | bytes 884744 | tf_op jit(solution)/shard_map/ppermute | solution.py:46
  12.2 3.1 %collective-permute-start.3 = (bf16[6,192,128]{2,1,0:T(8,128)(2,1)S(1)}, bf16[6,192,128]{2,1,0:T(8,128)(2,1)S(1)}, u32[]{:S(2)}, u32[]{:S(2)}) collective-permute-start(bf16[6,192,128]{2,1,0:T(8,128)(2,1)S(1)} %get-tuple-element.29), channel_id=1, source_target_pairs={{0,1},{1,0},{2,3},{3,2},{4,5},{5,4},{6,7},{7,6},{8,9},{9,8},{10,11... | collective-permute-start | bytes 884744 | tf_op jit(solution)/shard_map/ppermute | solution.py:46
  15.3 0.0 collective-permute-done.early
  15.3 0.0 collective-permute-done.1.late
  15.3 0.3 split.1
  15.6 2.4 %collective-permute-start.4 = (bf16[5,208,128]{2,1,0:T(8,128)(2,1)S(1)}, bf16[5,208,128]{2,1,0:T(8,128)(2,1)S(1)}, u32[]{:S(2)}, u32[]{:S(2)}) collective-permute-start(bf16[5,208,128]{2,1,0:T(8,128)(2,1)S(1)} %get-tuple-element.31), channel_id=1, source_target_pairs={{1,2},{2,1},{3,4},{4,3},{5,6},{6,5},{7,8},{8,7},{9,10},{10,9},{11,... | collective-permute-start | bytes 798728 | tf_op jit(solution)/shard_map/ppermute | solution.py:46
  18.1 4.5 %collective-permute-start.5 = (bf16[5,208,128]{2,1,0:T(8,128)(2,1)S(1)}, bf16[5,208,128]{2,1,0:T(8,128)(2,1)S(1)}, u32[]{:S(2)}, u32[]{:S(2)}) collective-permute-start(bf16[5,208,128]{2,1,0:T(8,128)(2,1)S(1)} %get-tuple-element.32), channel_id=1, source_target_pairs={{0,1},{1,0},{2,3},{3,2},{4,5},{5,4},{6,7},{7,6},{8,9},{9,8},{10,11... | collective-permute-start | bytes 798728 | tf_op jit(solution)/shard_map/ppermute | solution.py:46
  22.6 1.1 %toeplitz.1 = (bf16[6,576,256]{2,1,0:T(8,128)(2,1)S(1)}, f32[48,256]{1,0:T(8,128)S(1)}, bf16[6,384,384]{2,1,0:T(8,128)(2,1)S(1)}) custom-call(f32[6,3,201]{2,1,0:T(4,128)S(1)} %get-tuple-element.33.row_ref, f32[6,3,201]{2,1,0:T(4,128)S(1)} %get-tuple-element.34.col_ref), custom_call_target="tpu_custom_call" | custom-call | bytes 8000000 | tf_op jit(solution)/shard_map/toeplitz/pallas_call | solution.py:224
  23.7 0.0 collective-permute-done.2.outer
  23.7 0.0 collective-permute-done.3.inner
  23.7 2.2 %own_part.1 = (f32[6,192,768]{2,1,0:T(8,128)S(1)}, f32[6,208,768]{2,1,0:T(8,128)S(1)}, bf16[6,576,256]{2,1,0:T(8,128)(2,1)S(1)}) custom-call(bf16[6,400,256]{2,1,0:T(8,128)(2,1)S(1)} %get-tuple-element.27.field, bf16[6,192,128]{2,1,0:T(8,128)(2,1)S(1)} %collective-permute-done.2.outer, bf16[6,192,128]{2,1,0:T(8,128)(2,1)S(1)} %collective-permute-done.3.inner, ...), custom_call_target="tpu_custom_call" | custom-call | flops 1849688064 | bytes 10000000 | tf_op jit(solution)/shard_map/own_part/pallas_call | solution.py:360
  25.9 0.0 collective-permute-done.4.far_outer
  25.9 0.0 collective-permute-done.5.far_inner
  26.0 2.3 %last_part.1 = f32[6,192,256]{2,1,0:T(8,128)} custom-call(f32[16,256]{1,0:T(8,128)S(1)} %get-tuple-element.23.scales, bf16[6,400,256]{2,1,0:T(8,128)(2,1)S(1)} %get-tuple-element.27.field, bf16[6,192,128]{2,1,0:T(8,128)(2,1)S(1)} %collective-permute-done.2.outer, bf16[6,192,128]{2,1,0:T(8,128)(2,1)S(1)} %collective-permute-done.3.inner, ...), custom_call_target="tpu_custom_call" | custom-call | flops 943718400 | bytes 12000000 | tf_op jit(solution)/shard_map/last_part/pallas_call | solution.py:522
Async XLA Ops:
  1.4 13.9 %collective-permute-start = (bf16[6,104,256]{2,1,0:T(8,128)(2,1)S(1)}, bf16[6,104,256]{2,1,0:T(8,128)(2,1)S(1)}, u32[]{:S(2)}, u32[]{:S(2)}) collective-permute-start(bf16[6,104,256]{2,1,0:T(8,128)(2,1)S(1)} %get-tuple-element.25), channel_id=1, source_target_pairs={{1,33},{3,35},{5,37},{7,39},{9,41},{11,43},{13,45},{15,47},{17,49}... | collective-permute-start | bytes 958472 | tf_op jit(solution)/shard_map/ppermute | solution.py:38
  6.2 9.2 %collective-permute-start.1 = (bf16[6,104,256]{2,1,0:T(8,128)(2,1)S(1)}, bf16[6,104,256]{2,1,0:T(8,128)(2,1)S(1)}, u32[]{:S(2)}, u32[]{:S(2)}) collective-permute-start(bf16[6,104,256]{2,1,0:T(8,128)(2,1)S(1)} %get-tuple-element.26), channel_id=1, source_target_pairs={{0,32},{2,34},{4,36},{6,38},{8,40},{10,42},{12,44},{14,46},{16,48}... | collective-permute-start | bytes 958472 | tf_op jit(solution)/shard_map/ppermute | solution.py:38
  8.1 15.6 %collective-permute-start.2 = (bf16[6,192,128]{2,1,0:T(8,128)(2,1)S(1)}, bf16[6,192,128]{2,1,0:T(8,128)(2,1)S(1)}, u32[]{:S(2)}, u32[]{:S(2)}) collective-permute-start(bf16[6,192,128]{2,1,0:T(8,128)(2,1)S(1)} %get-tuple-element.28), channel_id=1, source_target_pairs={{1,2},{2,1},{3,4},{4,3},{5,6},{6,5},{7,8},{8,7},{9,10},{10,9},{11,... | collective-permute-start | bytes 884744 | tf_op jit(solution)/shard_map/ppermute | solution.py:46
  12.2 11.5 %collective-permute-start.3 = (bf16[6,192,128]{2,1,0:T(8,128)(2,1)S(1)}, bf16[6,192,128]{2,1,0:T(8,128)(2,1)S(1)}, u32[]{:S(2)}, u32[]{:S(2)}) collective-permute-start(bf16[6,192,128]{2,1,0:T(8,128)(2,1)S(1)} %get-tuple-element.29), channel_id=1, source_target_pairs={{0,1},{1,0},{2,3},{3,2},{4,5},{5,4},{6,7},{7,6},{8,9},{9,8},{10,11... | collective-permute-start | bytes 884744 | tf_op jit(solution)/shard_map/ppermute | solution.py:46
  15.6 10.3 %collective-permute-start.4 = (bf16[5,208,128]{2,1,0:T(8,128)(2,1)S(1)}, bf16[5,208,128]{2,1,0:T(8,128)(2,1)S(1)}, u32[]{:S(2)}, u32[]{:S(2)}) collective-permute-start(bf16[5,208,128]{2,1,0:T(8,128)(2,1)S(1)} %get-tuple-element.31), channel_id=1, source_target_pairs={{1,2},{2,1},{3,4},{4,3},{5,6},{6,5},{7,8},{8,7},{9,10},{10,9},{11,... | collective-permute-start | bytes 798728 | tf_op jit(solution)/shard_map/ppermute | solution.py:46
  18.1 7.9 %collective-permute-start.5 = (bf16[5,208,128]{2,1,0:T(8,128)(2,1)S(1)}, bf16[5,208,128]{2,1,0:T(8,128)(2,1)S(1)}, u32[]{:S(2)}, u32[]{:S(2)}) collective-permute-start(bf16[5,208,128]{2,1,0:T(8,128)(2,1)S(1)} %get-tuple-element.32), channel_id=1, source_target_pairs={{0,1},{1,0},{2,3},{3,2},{4,5},{5,4},{6,7},{7,6},{8,9},{9,8},{10,11... | collective-permute-start | bytes 798728 | tf_op jit(solution)/shard_map/ppermute | solution.py:46
